TPU v7x, 128 devices: a whole 4x4x4 slice. The times are simulated.
128 devices in a mesh: ctx: 16 (over z, x), head: 8 (over y, core).
Axes of the slice: x: 4, y: 4, z: 4, core: 2. Of those that a mesh axis runs over, the one named last changes fastest.
Arguments:
- tokens: bfloat16 [32768, 2048], P('ctx'), may hold values from -6 to 6
- project_weight: bfloat16 [2048, 3, 4096], P(None, None, 'head'), may hold values from -0.125 to 0.125
- level_weight: bfloat16 [32, 128, 17], P('head'), may hold values from -0.5 to 0.5
- norm_gain: float32 [4096], P('head'), may hold values from 0.25 to 1.75
- output_weight: bfloat16 [4096, 2048], P('head'), may hold values from -0.09375 to 0.09375
Outputs:
- layer_out: bfloat16 [32768, 2048], P('ctx', 'head')
All inputs are finite; a program needn't handle non-finite values.
Results may differ from a plain program's by a relative error of at most 0.015.
Values may be sent and summed in bfloat16 or wider, within the bound.
No kernel may reach another device: no remote copies, remote signals or barrier semaphores. Data moves between devices by JAX's collectives and lax.ppermute only.
A program may use at most 128 MiB of HBM per device.

v0:
```python
import functools

import jax
import jax.numpy as jnp
from jax import lax
from jax.experimental import pallas as pl
from jax.experimental.pallas import tpu as pltpu
from jax.sharding import PartitionSpec as P

BF16 = jnp.bfloat16
F32 = jnp.float32
BLOCK = 512
CHUNK = 256
TILE = 128
KV = 28
SMALL = 4


def dot(a, b):
    return jnp.dot(a, b, preferred_element_type=F32)


def dot_nt(a, b):
    return lax.dot_general(a, b, (((1,), (1,)), ((), ())), preferred_element_type=F32)


def cost(flops, mib):
    return pl.CostEstimate(flops=flops, bytes_accessed=mib << 20, transcendentals=0)


def bits_of(number):
    return sum((number >= 2**j).astype(jnp.int32) for j in range(4))


def key_value_block(heads, dim, block, rows, wk, wv, k_out, vt_out, chunk_out, total, keys=None):
    at = slice(block * BLOCK, (block + 1) * BLOCK)
    if keys is None:
        keys = dot(rows, wk[...])
    keys = keys.astype(BF16)
    k_out[at] = keys
    values = dot(rows, wv[...]).astype(BF16)
    for head in range(heads):
        cols = slice(head * dim, (head + 1) * dim)
        turned = values[:, cols].T
        vt_out[block, cols] = turned
        sums = None if block == 0 else total[head]
        for chunk in range(2):
            inner = slice(chunk * CHUNK, (chunk + 1) * CHUNK)
            state = dot(turned[:, inner], keys[inner, cols])
            chunk_out[2 * block + chunk, head] = state.astype(BF16)
            sums = state if sums is None else sums + state
        total[head] = sums


def first_kernel(heads, dim, tok_in, w_in, k_out, vt_out, chunk_out, total_out, tok, wq, wk, wv, total, sems):
    depth = tok.shape[1]
    part = depth // 2
    blocks = k_out.shape[0] // BLOCK
    head_rows = pl.ds(0, BLOCK)
    pairs = []
    for j in range(2):
        at = pl.ds(j * part, part)
        pairs.append((w_in.at[1, at], wk.at[at]))
        pairs.append((tok_in.at[head_rows, at], tok.at[head_rows, at]))
    pairs.append((w_in.at[2], wv))
    rest = pl.ds(BLOCK, tok.shape[0] - BLOCK)
    pairs.append((tok_in.at[rest], tok.at[rest]))
    pairs.append((w_in.at[0], wq))
    copies = [pltpu.make_async_copy(*pair, sems.at[j]) for j, pair in enumerate(pairs)]
    for copy in copies[:4]:
        copy.start()
    keys = None
    for j in range(2):
        copies[2 * j].wait()
        copies[2 * j + 1].wait()
        for copy in copies[4 + j : 5 + 2 * j]:
            copy.start()
        at = slice(j * part, (j + 1) * part)
        term = dot(tok[:BLOCK, at], wk[at])
        keys = term if keys is None else keys + term
    copies[4].wait()
    outs = (wk, wv, k_out, vt_out, chunk_out, total)
    key_value_block(heads, dim, 0, tok[:BLOCK], *outs, keys)
    copies[5].wait()
    for block in range(1, blocks):
        key_value_block(heads, dim, block, tok[block * BLOCK : (block + 1) * BLOCK], *outs)
    copies[6].wait()
    total_out[...] = total[...].astype(BF16)


def second_kernel(heads, dim, tok, wk, wv, k_out, vt_out, chunk_out, total_out, total):
    half = tok.shape[0] // 2
    for block in range(half // BLOCK):
        at = slice(half + block * BLOCK, half + (block + 1) * BLOCK)
        key_value_block(heads, dim, block, tok[at], wk, wv, k_out, vt_out, chunk_out, total)
    total_out[...] = total[...].astype(BF16)


def key_value(heads, dim, rows, args, first):
    depth = args[0].shape[1]
    width = heads * dim
    vmem = pl.BlockSpec(memory_space=pltpu.VMEM)
    shapes = [
        jax.ShapeDtypeStruct((rows, width), BF16),
        jax.ShapeDtypeStruct((rows // BLOCK, width, BLOCK), BF16),
        jax.ShapeDtypeStruct((rows // CHUNK, heads, dim, dim), BF16),
        jax.ShapeDtypeStruct((heads, dim, dim), BF16),
    ]
    scratch = [pltpu.VMEM((heads, dim, dim), F32)]
    if first:
        shapes.append(jax.ShapeDtypeStruct(args[0].shape, BF16))
        shapes += [jax.ShapeDtypeStruct((depth, width), BF16)] * 3
        scratch.append(pltpu.SemaphoreType.DMA((7,)))
    return pl.pallas_call(
        functools.partial(first_kernel if first else second_kernel, heads, dim),
        in_specs=[pl.BlockSpec(memory_space=pltpu.HBM)] * 2 if first else [vmem] * 3,
        out_specs=[vmem] * len(shapes),
        out_shape=shapes,
        scratch_shapes=scratch,
        compiler_params=pltpu.CompilerParams(vmem_limit_bytes=(KV if first else SMALL) << 20),
        cost_estimate=cost(4 * rows * depth * width, 14),
        name="key_value",
    )(*args)


def sums_kernel(*refs):
    count = len(refs) // 3
    for j in range(count):
        refs[2 * count + j][...] = (refs[2 * j][...].astype(F32) + refs[2 * j + 1][...].astype(F32)).astype(BF16)


def added(*pairs):
    vmem = pl.BlockSpec(memory_space=pltpu.VMEM)
    flat = [value for pair in pairs for value in pair]
    return pl.pallas_call(
        sums_kernel,
        in_specs=[vmem] * len(flat),
        out_specs=[vmem] * len(pairs),
        out_shape=[jax.ShapeDtypeStruct(pair[0].shape, BF16) for pair in pairs],
        compiler_params=pltpu.CompilerParams(vmem_limit_bytes=SMALL << 20),
        cost_estimate=cost(1 << 18, 1),
        name="added",
    )(*flat)


def near_kernel(
    heads, dim, half, step, tok, wq, keys, vt, states, level_w, after, near_out, q_out, coef_out, steps_ref
):
    del after
    first = half * (tok.shape[0] // 2) + step * BLOCK
    k_ref = keys.at[pl.ds(step * BLOCK, BLOCK)]
    vt_ref = vt.at[step]
    queries = dot(tok[first : first + BLOCK], wq[...]).astype(BF16)
    q_out[...] = queries
    levels = level_w.shape[0]
    count = levels * heads
    flat = level_w[...].astype(F32).reshape(count, dim)
    owner = lax.broadcasted_iota(jnp.int32, (count, heads * dim), 0) % heads
    lane_head = lax.broadcasted_iota(jnp.int32, (count, heads * dim), 1) // dim
    gate_w = jnp.where(owner == lane_head, jnp.concatenate([flat] * heads, axis=1), 0.0)
    logits = dot_nt(gate_w.astype(BF16), queries)
    gate = jnp.maximum(logits, 0.0) + jnp.log1p(jnp.exp(-jnp.abs(logits)))
    level_at = lax.broadcasted_iota(jnp.int32, logits.shape, 0) // heads
    coef_out[...] = gate * jnp.exp2(-0.5 * level_at.astype(F32))

    def row(head, level, count, at=slice(None)):
        return coef_out[pl.ds(level * heads + head, count, stride=0), :][:, at]

    lane = lax.broadcasted_iota(jnp.int32, (16, BLOCK), 1)
    group = lax.broadcasted_iota(jnp.int32, (16, BLOCK), 0)
    query_group = jnp.bitwise_and(lane, TILE - 1) // 8
    apart = bits_of(jnp.bitwise_xor(query_group, group))
    before = query_group > group
    lane8 = jnp.bitwise_and(lane[:8], 7)
    key8 = group[:8]
    near8 = bits_of(jnp.bitwise_xor(lane8, key8))
    causal8 = lane8 >= key8
    tile_group = jnp.bitwise_and(lax.broadcasted_iota(jnp.int32, (8, CHUNK), 1), TILE - 1) // 8
    for head in range(heads):
        cols = slice(head * dim, (head + 1) * dim)
        rough = jnp.zeros((16, BLOCK), F32)
        for level in range(1, 5):
            rough = jnp.where(apart == level, row(head, level + 3, 16), rough)
        steps_ref[...] = jnp.where(before, rough, 0.0)
        fine = row(head, 0, 8)
        for level in range(1, 4):
            fine = jnp.where(near8 == level, row(head, level, 8), fine)
        fine = jnp.where(causal8, fine, 0.0)
        pair = (states[0, head].astype(F32) + states[1, head].astype(F32)).astype(BF16)
        for chunk in range(2):
            at = slice(chunk * CHUNK, (chunk + 1) * CHUNK)
            query = queries[at, cols]
            left = [k_ref[at, cols]]
            if step == 1:
                left.append(pair)
            if chunk == 1:
                left.append(states[2 * step, head])
            score = dot_nt(jnp.concatenate(left, axis=0), query)
            top, bottom = [], []
            across = row(head, 8, 8, slice(chunk * CHUNK + TILE, (chunk + 1) * CHUNK))
            for j in range(16):
                weight = jnp.where(
                    tile_group == j, fine[:, at], steps_ref[pl.ds(j, 8, stride=0), :][:, at]
                )
                low = score[8 * j : 8 * j + 8]
                high = score[TILE + 8 * j : TILE + 8 * j + 8, TILE:]
                top.append(
                    jnp.concatenate([low[:, :TILE] * weight[:, :TILE], low[:, TILE:] * across], axis=1)
                )
                bottom.append(
                    jnp.concatenate([jnp.zeros((8, TILE), F32), high * weight[:, TILE:]], axis=1)
                )
            mixed = jnp.concatenate(top + bottom, axis=0).astype(BF16)
            near = dot(vt_ref[cols, at], mixed)
            wider = ([10] if step == 1 else []) + ([9] if chunk == 1 else [])
            for order, level in enumerate(wider):
                scale = jnp.concatenate([row(head, level, 8, at)] * (dim // 8), axis=0)
                near = near + scale * score[CHUNK + order * dim : CHUNK + (order + 1) * dim]
            near_out[cols, at] = near


def near_part(held, after, half, step, heads, dim):
    depth = held[0].shape[1]
    width = heads * dim
    vmem = pl.BlockSpec(memory_space=pltpu.VMEM)
    return pl.pallas_call(
        functools.partial(near_kernel, heads, dim, half, step),
        in_specs=[vmem] * 6 + [pl.BlockSpec(memory_space=pl.ANY)],
        out_specs=[vmem] * 3,
        out_shape=[
            jax.ShapeDtypeStruct((width, BLOCK), F32),
            jax.ShapeDtypeStruct((BLOCK, width), BF16),
            jax.ShapeDtypeStruct((held[5].shape[0] * heads, BLOCK), F32),
        ],
        scratch_shapes=[pltpu.VMEM((16, BLOCK), F32)],
        compiler_params=pltpu.CompilerParams(vmem_limit_bytes=SMALL << 20),
        cost_estimate=cost(4 * BLOCK * depth * width, 14),
        name="near_part",
    )(*held, after)


def far_kernel(heads, dim, level0, count, half, device, after, gain, *refs):
    del after
    bits = [(device[0] >> level) & 1 for level in range(4)]
    flags = [(bit if half == 0 else 1 - bit).astype(F32) for bit in bits]
    blocks = (len(refs) - count - 2) // 3
    states, (out, gains) = refs[3 * blocks : -2], refs[-2:]
    for head in range(heads):
        cols = slice(head * dim, (head + 1) * dim)
        gains[cols] = jnp.broadcast_to(gain[:, cols], (dim, dim)).T
    for block in range(blocks):
        near, q_ref, coef_ref = refs[3 * block : 3 * block + 3]
        for head in range(heads):
            cols = slice(head * dim, (head + 1) * dim)
            far = jnp.concatenate([state[head] for state in states], axis=0)
            for chunk in range(2):
                at = slice(chunk * CHUNK, (chunk + 1) * CHUNK)
                terms = dot_nt(far, q_ref[at, cols])
                acc = near[cols, at]
                for level in range(count):
                    lane = (level0 + level) * heads + head
                    scale = coef_ref[pl.ds(lane, 8, stride=0), :][:, at]
                    if level < 4:
                        scale = scale * flags[level]
                    scale = jnp.concatenate([scale] * (dim // 8), axis=0)
                    acc = acc + scale * terms[level * dim : (level + 1) * dim]
                mean = jnp.mean(acc * acc, axis=0, keepdims=True)
                both = jnp.concatenate([gains[cols], gains[cols]], axis=1)
                rows = slice(block * BLOCK + chunk * CHUNK, block * BLOCK + (chunk + 1) * CHUNK)
                out[rows, cols] = (acc * lax.rsqrt(mean + 1e-06) * both).astype(BF16).T


def far_part(device, after, near, gain, states, heads, dim, level0):
    rows = len(near) * BLOCK
    width = heads * dim
    count = len(states)
    blocks = [part for block in near for part in block]
    vmem = pl.BlockSpec(memory_space=pltpu.VMEM)
    return pl.pallas_call(
        functools.partial(far_kernel, heads, dim, level0, count, count - 4),
        in_specs=[pl.BlockSpec(memory_space=pltpu.SMEM), pl.BlockSpec(memory_space=pl.ANY)]
        + [vmem] * (1 + len(blocks) + count),
        out_specs=vmem,
        out_shape=jax.ShapeDtypeStruct((rows, width), BF16),
        scratch_shapes=[pltpu.VMEM((width, dim), F32)],
        compiler_params=pltpu.CompilerParams(vmem_limit_bytes=SMALL << 20),
        cost_estimate=cost(2 * rows * dim * width * count, 5),
        name="far_part",
    )(device, after, gain, *blocks, *states)


def project_kernel(feats, ring, group, own, peer, w_own, w_peer, top, bottom, up, down, mine):
    block = own.shape[0] // 2
    for order, shift in enumerate((2, 1, ring - 1, 0)):
        slot = 2 * (((group[0] >> 1) + shift) % ring) + (group[0] & 1)
        at = pl.ds(pl.multiple_of(slot * feats, feats), feats)
        for part in range(2):
            rows = slice(part * block, (part + 1) * block)
            total = dot(own[rows], w_own[:, at]) + dot(peer[rows], w_peer[:, at])
            if order == 0:
                (top, bottom)[part][...] = total.astype(BF16)
            else:
                out = (up, down, mine)[order - 1]
                out[rows] = total.astype(out.dtype)


def project(group, ring, own, peer, w_own, w_peer, feats):
    rows, width = own.shape
    vmem = pl.BlockSpec(memory_space=pltpu.VMEM)
    return pl.pallas_call(
        functools.partial(project_kernel, feats, ring),
        in_specs=[pl.BlockSpec(memory_space=pltpu.SMEM)] + [vmem] * 4,
        out_specs=[vmem] * 5,
        out_shape=[jax.ShapeDtypeStruct((rows // 2, feats), BF16)] * 2
        + [jax.ShapeDtypeStruct((rows, feats), BF16)] * 2
        + [jax.ShapeDtypeStruct((rows, feats), F32)],
        compiler_params=pltpu.CompilerParams(vmem_limit_bytes=12 << 20),
        cost_estimate=cost(16 * rows * width * feats, 4),
        name="project",
    )(group, own, peer, w_own, w_peer)


def relay_kernel(up_in, down_in, from_down, from_up, after, up, down):
    del after
    block = from_down.shape[0]
    up[:block] = (up_in[:block].astype(F32) + from_down[...].astype(F32)).astype(BF16)
    up[block:] = up_in[block:]
    down[:block] = down_in[:block]
    down[block:] = (down_in[block:].astype(F32) + from_up[...].astype(F32)).astype(BF16)


def relay(up, down, from_down, from_up, after):
    vmem = pl.BlockSpec(memory_space=pltpu.VMEM)
    return pl.pallas_call(
        relay_kernel,
        in_specs=[vmem] * 4 + [pl.BlockSpec(memory_space=pl.ANY)],
        out_specs=[vmem] * 2,
        out_shape=[jax.ShapeDtypeStruct(up.shape, BF16)] * 2,
        compiler_params=pltpu.CompilerParams(vmem_limit_bytes=SMALL << 20),
        cost_estimate=cost(1 << 18, 1),
        name="relay",
    )(up, down, from_down, from_up, after)


def shards(tokens, project_weight, level_weight, norm_gain, output_weight):
    heads, dim, _ = level_weight.shape
    half_rows = tokens.shape[0] // 2
    ctx_count = lax.axis_size("ctx")
    head_count = lax.axis_size("head")
    feats = output_weight.shape[1] // head_count
    device = lax.axis_index("ctx")
    group = lax.axis_index("head")
    ring = head_count // 2
    level0 = half_rows.bit_length()

    def over_core(value):
        return lax.ppermute(value, "head", [(i, i ^ 1) for i in range(head_count)])

    def over_ring(value, shift):
        return lax.ppermute(
            value, "head", [(i, (i + 2 * shift) % head_count) for i in range(head_count)]
        )

    weights = jnp.transpose(project_weight, (1, 0, 2))
    peer_weight = over_core(output_weight)
    gate_w = jnp.transpose(level_weight, (2, 0, 1))
    gain = norm_gain[None]
    tokens, where_ctx, where_head = lax.optimization_barrier(
        (tokens, device.reshape(1), group.reshape(1))
    )

    def over_ctx(value, mask):
        return lax.ppermute(value, "ctx", [(i, i ^ mask) for i in range(ctx_count)])

    low = key_value(heads, dim, half_rows, (tokens, weights), True)
    rows, weight_q, weight_k, weight_v = low[4:]
    held = [None, None]
    held[0] = (rows, weight_q, *low[:3], gate_w)
    sums = [low[3], None]
    levels_of = [[], []]

    def step_of(half, mask):
        return over_ctx(sums[half], mask)

    def advance(**arrived):
        names = {"low": 0, "high": 1}
        fresh = added(*[(sums[names[name]], value) for name, value in arrived.items()])
        for (name, value), total in zip(arrived.items(), fresh):
            levels_of[names[name]].append(value)
            sums[names[name]] = total

    near = {}
    masks = (1, 3, 4, 12)
    low_x1 = step_of(0, masks[0])
    high = key_value(heads, dim, half_rows, (rows, weight_k, weight_v), False)
    held[1] = (rows, weight_q, *high[:3], gate_w)
    sums[1] = high[3]
    low_x1, sums[1] = lax.optimization_barrier((low_x1, sums[1]))
    advance(low=low_x1)
    low_x3, high_x1 = step_of(0, masks[1]), step_of(1, masks[0])

    def block_after(half, step, value):
        start, *others = held[half]
        start, value = lax.optimization_barrier((start, value))
        near[half, step] = near_part((start, *others), value, half, step, heads, dim)
        return value

    sums[0] = block_after(0, 0, sums[0])
    low_x3, high_x1, near[0, 0] = lax.optimization_barrier((low_x3, high_x1, near[0, 0]))
    advance(low=low_x3, high=high_x1)
    low_z1, high_x3 = step_of(0, masks[2]), step_of(1, masks[1])
    sums[0] = block_after(0, 1, sums[0])
    low_z1, high_x3, near[0, 1] = lax.optimization_barrier((low_z1, high_x3, near[0, 1]))
    advance(low=low_z1, high=high_x3)
    low_z3, high_z1 = step_of(0, masks[3]), step_of(1, masks[2])
    sums[0] = block_after(1, 0, sums[0])
    low_z3, high_z1, near[1, 0] = lax.optimization_barrier((low_z3, high_z1, near[1, 0]))
    advance(low=low_z3, high=high_z1)
    high_z3 = step_of(1, masks[3])
    levels_of[1].append(high_z3)
    levels_of[1].append(sums[0])

    def joined(*terms):
        return functools.reduce(jnp.add, [term.astype(F32) for term in terms]).astype(BF16)

    def attended(half, after):
        parts = [near[half, 0], near[half, 1]]
        return far_part(where_ctx, after, parts, gain, levels_of[half], heads, dim, level0)

    def sent(own, peer):
        return project(where_head, ring, own, peer, output_weight, peer_weight, feats)

    own_low = attended(0, sums[0])
    peer_low = over_core(own_low)
    near[1, 1] = near_part(held[1], own_low, 1, 1, heads, dim)
    sends = [sent(own_low, peer_low)]
    own_high = attended(1, sends[0][0])
    sends.append(sent(own_high, over_core(own_high)))
    results = []

    low_pair = [over_ring(sends[0][0], 1), over_ring(sends[0][1], -1)]
    high_pair = [over_ring(sends[1][0], 1), over_ring(sends[1][1], -1)]
    arrived = [low_pair, high_pair]
    for half in range(2):
        up, down, mine = sends[half][2:]
        make = lambda: relay(up, down, *arrived[half], sends[1][0])
        up, down = make()
        results.append(joined(mine, over_ring(up, 1), over_ring(down, -1)))
    return jnp.concatenate(results, axis=0)


def solution(mesh):
    placed = (
        P("ctx", None),
        P(None, None, "head"),
        P("head", None, None),
        P("head"),
        P("head", None),
    )
    return jax.shard_map(
        shards, mesh=mesh, in_specs=placed, out_specs=P("ctx", "head"), check_vma=False
    )
```

profile of v0, /device:TPU:0, one launch (start us, length us, event | category | flops | bytes accessed | tf_op | source)
XLA Modules:
  0.0 98.7 jit_solution(1337740205189138240)
XLA Ops:
  0.0 2.8 %copy-done.2 = bf16[2048,3,512]{2,0,1:T(8,128)(2,1)S(1)} copy-done((bf16[2048,3,512]{2,0,1:T(8,128)(2,1)S(1)}, bf16[2048,3,512]{2,0,1:T(8,128)(2,1)}, u32[]{:S(2)}) %copy-start.2) | copy-done | bytes 6291480
  2.8 7.4 %key_value.2 = (bf16[1024,512]{1,0:T(8,128)(2,1)S(1)}, bf16[2,512,512]{2,1,0:T(8,128)(2,1)S(1)}, bf16[4,4,128,128]{3,2,1,0:T(8,128)(2,1)S(1)}, bf16[4,128,128]{2...) custom-call(bf16[2048,2048]{1,0:T(8,128)(2,1)} %tok_in, ...), custom_call_target="tpu_custom_call" | custom-call | flops 4294967296 | bytes 14680064 | tf_op jit(solution)/shard_map/key_value/pallas_call | solution.py:114
  10.2 1.7 %collective-permute-start = (bf16[4,128,128]{2,1,0:T(8,128)(2,1)S(1)}, bf16[4,128,128]{2,1,0:T(8,128)(2,1)S(1)}, u32[]{:S(2)}, u32[]{:S(2)}) collective-permute-start(bf16[4,128,128]{2,1,0:T(8,128)(2,1)S(1)} %get-tuple-element.79.refs_0_), channel_id=1, source_target_pairs={{0,8},{8,0},{16,24},{24,16},{32,40},{40,32},{48,56},{56,48},{64,72... | collective-permute-start | bytes 393224 | tf_op jit(solution)/shard_map/ppermute | solution.py:373
  11.9 0.0 collective-permute-start.8
  11.9 5.0 %key_value.3 = (bf16[1024,512]{1,0:T(8,128)(2,1)S(1)}, bf16[2,512,512]{2,1,0:T(8,128)(2,1)S(1)}, bf16[4,4,128,128]{3,2,1,0:T(8,128)(2,1)S(1)}, bf16[4,128,128]{2,1,0:T(8,128)(2,1)S(1)}) custom-call(bf16[2048,2048]{1,0:T(8,128)(2,1)S(1)} %get-tuple-element.108.tok, bf16[2048,512]{1,0:T(8,128)(2,1)S(1)} %get-tuple-element.80.wk, ...), custom_call_target="tpu_custom_call" | custom-call | flops 4294967296 | bytes 14680064 | tf_op jit(solution)/shard_map/key_value/pallas_call | solution.py:114
  17.0 0.0 collective-permute-done.refs_1_.refs_6_
  17.0 2.2 %collective-permute-start.1 = (bf16[4,128,128]{2,1,0:T(8,128)(2,1)S(1)}, bf16[4,128,128]{2,1,0:T(8,128)(2,1)S(1)}, u32[]{:S(2)}, u32[]{:S(2)}) collective-permute-start(bf16[4,128,128]{2,1,0:T(8,128)(2,1)S(1)} %added.4.after.refs_0_), channel_id=1, source_target_pairs={{0,24},{8,16},{16,8},{24,0},{32,56},{40,48},{48,40},{56,32},{64,88... | collective-permute-start | bytes 393224 | tf_op jit(solution)/shard_map/ppermute | solution.py:373
  19.2 0.6 collective-permute-start.2
  19.8 2.7 %near_part.4 = (f32[512,512]{1,0:T(8,128)S(1)}, bf16[512,512]{1,0:T(8,128)(2,1)S(1)}, f32[68,512]{1,0:T(8,128)S(1)}) custom-call(bf16[2048,2048]{1,0:T(8,128)(2,1)S(1)} %get-tuple-element.108.tok, bf16[2048,512]{1,0:T(8,128)(2,1)S(1)} %get-tuple-element.87.wq, bf16[1024,512]{1,0:T(8,128)(2,1)S(1)} %get-tuple-element.88.keys, ...), custom_call_target="tpu_custom_call" | custom-call | flops 2147483648 | bytes 14680064 | tf_op jit(solution)/shard_map/near_part/pallas_call | solution.py:226
  22.5 1.7 %collective-permute-done.1.refs_1_.refs_7_ = bf16[4,128,128]{2,1,0:T(8,128)(2,1)S(1)} collective-permute-done((bf16[4,128,128]{2,1,0:T(8,128)(2,1)S(1)}, bf16[4,128,128]{2,1,0:T(8,128)(2,1)S(1)}, u32[]{:S(2)}, u32[]{:S(2)}) %collective-permute-start.1) | collective-permute-done | bytes 131104 | tf_op jit(solution)/shard_map/ppermute | solution.py:373
  24.2 0.6 collective-permute-done.2.refs_3_.refs_6_
  24.8 0.1 added.5
  24.9 2.0 %collective-permute-start.3 = (bf16[4,128,128]{2,1,0:T(8,128)(2,1)S(1)}, bf16[4,128,128]{2,1,0:T(8,128)(2,1)S(1)}, u32[]{:S(2)}, u32[]{:S(2)}) collective-permute-start(bf16[4,128,128]{2,1,0:T(8,128)(2,1)S(1)} %get-tuple-element.97.after.refs_0_), channel_id=1, source_target_pairs={{0,32},{8,40},{16,48},{24,56},{32,0},{40,8},{48,16},{56,24},{64,96... | collective-permute-start | bytes 393224 | tf_op jit(solution)/shard_map/ppermute | solution.py:373
  26.9 1.5 %collective-permute-start.4 = (bf16[4,128,128]{2,1,0:T(8,128)(2,1)S(1)}, bf16[4,128,128]{2,1,0:T(8,128)(2,1)S(1)}, u32[]{:S(2)}, u32[]{:S(2)}) collective-permute-start(bf16[4,128,128]{2,1,0:T(8,128)(2,1)S(1)} %get-tuple-element.98.refs_2_), channel_id=1, source_target_pairs={{0,24},{8,16},{16,8},{24,0},{32,56},{40,48},{48,40},{56,32},{64,88... | collective-permute-start | bytes 393224 | tf_op jit(solution)/shard_map/ppermute | solution.py:373
  28.4 2.9 %near_part.5 = (f32[512,512]{1,0:T(8,128)S(1)}, bf16[512,512]{1,0:T(8,128)(2,1)S(1)}, f32[68,512]{1,0:T(8,128)S(1)}) custom-call(bf16[2048,2048]{1,0:T(8,128)(2,1)S(1)} %get-tuple-element.108.tok, bf16[2048,512]{1,0:T(8,128)(2,1)S(1)} %get-tuple-element.87.wq, bf16[1024,512]{1,0:T(8,128)(2,1)S(1)} %get-tuple-element.88.keys, ...), custom_call_target="tpu_custom_call" | custom-call | flops 2147483648 | bytes 14680064 | tf_op jit(solution)/shard_map/near_part/pallas_call | solution.py:226
  31.3 0.0 collective-permute-done.3.refs_1_.refs_8_
  31.3 1.8 %collective-permute-done.4.refs_3_.refs_7_ = bf16[4,128,128]{2,1,0:T(8,128)(2,1)S(1)} collective-permute-done((bf16[4,128,128]{2,1,0:T(8,128)(2,1)S(1)}, bf16[4,128,128]{2,1,0:T(8,128)(2,1)S(1)}, u32[]{:S(2)}, u32[]{:S(2)}) %collective-permute-start.4) | collective-permute-done | bytes 131104 | tf_op jit(solution)/shard_map/ppermute | solution.py:373
  33.1 0.1 added.6
  33.1 2.6 %collective-permute-start.5 = (bf16[4,128,128]{2,1,0:T(8,128)(2,1)S(1)}, bf16[4,128,128]{2,1,0:T(8,128)(2,1)S(1)}, u32[]{:S(2)}, u32[]{:S(2)}) collective-permute-start(bf16[4,128,128]{2,1,0:T(8,128)(2,1)S(1)} %get-tuple-element.106.after.refs_0_), channel_id=1, source_target_pairs={{0,96},{8,104},{16,112},{24,120},{32,64},{40,72},{48,80},{56,88},{... | collective-permute-start | bytes 393224 | tf_op jit(solution)/shard_map/ppermute | solution.py:373
  35.8 1.0 %collective-permute-start.6 = (bf16[4,128,128]{2,1,0:T(8,128)(2,1)S(1)}, bf16[4,128,128]{2,1,0:T(8,128)(2,1)S(1)}, u32[]{:S(2)}, u32[]{:S(2)}) collective-permute-start(bf16[4,128,128]{2,1,0:T(8,128)(2,1)S(1)} %get-tuple-element.107.refs_2_), channel_id=1, source_target_pairs={{0,32},{8,40},{16,48},{24,56},{32,0},{40,8},{48,16},{56,24},{64,96... | collective-permute-start | bytes 393224 | tf_op jit(solution)/shard_map/ppermute | solution.py:373
  36.8 2.7 %near_part.6 = (f32[512,512]{1,0:T(8,128)S(1)}, bf16[512,512]{1,0:T(8,128)(2,1)S(1)}, f32[68,512]{1,0:T(8,128)S(1)}) custom-call(bf16[2048,2048]{1,0:T(8,128)(2,1)S(1)} %get-tuple-element.108.tok, bf16[2048,512]{1,0:T(8,128)(2,1)S(1)} %get-tuple-element.87.wq, bf16[1024,512]{1,0:T(8,128)(2,1)S(1)} %get-tuple-element.109.keys, ...), custom_call_target="tpu_custom_call" | custom-call | flops 2147483648 | bytes 14680064 | tf_op jit(solution)/shard_map/near_part/pallas_call | solution.py:226
  39.5 0.0 collective-permute-done.5.refs_1_.refs_9_
  39.5 1.2 %collective-permute-done.6.refs_3_.refs_8_ = bf16[4,128,128]{2,1,0:T(8,128)(2,1)S(1)} collective-permute-done((bf16[4,128,128]{2,1,0:T(8,128)(2,1)S(1)}, bf16[4,128,128]{2,1,0:T(8,128)(2,1)S(1)}, u32[]{:S(2)}, u32[]{:S(2)}) %collective-permute-start.6) | collective-permute-done | bytes 131104 | tf_op jit(solution)/shard_map/ppermute | solution.py:373
  40.7 0.1 added.7
  40.8 1.5 %far_part.2.own.after = bf16[1024,512]{1,0:T(8,128)(2,1)S(1)} custom-call(s32[1]{0:T(128)} %bitcast.device, bf16[4,128,128]{2,1,0:T(8,128)(2,1)S(1)} %get-tuple-element.117.after.refs_10_, f32[1,512]{1,0:T(1,128)S(1)} %bitcast.9, f32[512,512]{1,0:T(8,128)S(1)} %get-tuple-element.118.refs_0_, bf16[512,512]{1,0:T(8,128)(2,1)S(1)} %get-tuple-element.119.refs_1_, ...), custom_call_target="tpu_custom_call" | custom-call | flops 536870912 | bytes 5242880 | tf_op jit(solution)/shard_map/far_part/pallas_call | solution.py:279
  42.3 0.1 collective-permute-start.7
  42.4 1.3 %collective-permute-start.11 = (bf16[4,128,128]{2,1,0:T(8,128)(2,1)S(1)}, bf16[4,128,128]{2,1,0:T(8,128)(2,1)S(1)}, u32[]{:S(2)}, u32[]{:S(2)}) collective-permute-start(bf16[4,128,128]{2,1,0:T(8,128)(2,1)S(1)} %get-tuple-element.135), channel_id=1, source_target_pairs={{0,96},{8,104},{16,112},{24,120},{32,64},{40,72},{48,80},{56,88},{... | collective-permute-start | bytes 393224 | tf_op jit(solution)/shard_map/ppermute | solution.py:373
  43.7 2.9 %near_part.7 = (f32[512,512]{1,0:T(8,128)S(1)}, bf16[512,512]{1,0:T(8,128)(2,1)S(1)}, f32[68,512]{1,0:T(8,128)S(1)}) custom-call(bf16[2048,2048]{1,0:T(8,128)(2,1)S(1)} %get-tuple-element.108.tok, bf16[2048,512]{1,0:T(8,128)(2,1)S(1)} %get-tuple-element.87.wq, bf16[1024,512]{1,0:T(8,128)(2,1)S(1)} %get-tuple-element.109.keys, ...), custom_call_target="tpu_custom_call" | custom-call | flops 2147483648 | bytes 14680064 | tf_op jit(solution)/shard_map/near_part/pallas_call | solution.py:226
  46.6 2.4 %project.2 = (bf16[512,256]{1,0:T(8,128)(2,1)S(1)}, bf16[512,256]{1,0:T(8,128)(2,1)S(1)}, bf16[1024,256]{1,0:T(8,128)(2,1)S(1)}, bf16[1024,256]{1,0:T(8,128)(2,1)S(1)}, f32[1024,256]{1,0:T(8,128)S(1)}) custom-call(s32[1]{0:T(128)} %bitcast.1.group, bf16[1024,512]{1,0:T(8,128)(2,1)S(1)} %far_part.2.own.after, ...), custom_call_target="tpu_custom_call" | custom-call | flops 2147483648 | bytes 4194304 | tf_op jit(solution)/shard_map/project/pallas_call | solution.py:310
  48.9 0.6 collective-permute-done.11.refs_9_
  49.5 1.7 %far_part.3.own = bf16[1024,512]{1,0:T(8,128)(2,1)S(1)} custom-call(s32[1]{0:T(128)} %bitcast.device, bf16[512,256]{1,0:T(8,128)(2,1)S(1)} %get-tuple-element.127.after, f32[1,512]{1,0:T(1,128)S(1)} %bitcast.10, f32[512,512]{1,0:T(8,128)S(1)} %get-tuple-element.129.refs_0_, bf16[512,512]{1,0:T(8,128)(2,1)S(1)} %get-tuple-element.130.refs_1_, ...), custom_call_target="tpu_custom_call" | custom-call | flops 671088640 | bytes 5242880 | tf_op jit(solution)/shard_map/far_part/pallas_call | solution.py:279
  51.2 0.1 collective-permute-start.12
  51.3 3.3 %collective-permute-start.10 = (bf16[512,256]{1,0:T(8,128)(2,1)S(1)}, bf16[512,256]{1,0:T(8,128)(2,1)S(1)}, u32[]{:S(2)}, u32[]{:S(2)}) collective-permute-start(bf16[512,256]{1,0:T(8,128)(2,1)S(1)} %get-tuple-element.128), channel_id=1, source_target_pairs={{0,6},{1,7},{2,0},{3,1},{4,2},{5,3},{6,4},{7,5},{8,14},{9,15},{10,... | collective-permute-start | bytes 786440 | tf_op jit(solution)/shard_map/ppermute | solution.py:360
  54.6 2.4 %project.3 = (bf16[512,256]{1,0:T(8,128)(2,1)S(1)}, bf16[512,256]{1,0:T(8,128)(2,1)S(1)}, bf16[1024,256]{1,0:T(8,128)(2,1)S(1)}, bf16[1024,256]{1,0:T(8,128)(2,1)S(1)}, f32[1024,256]{1,0:T(8,128)S(1)}) custom-call(s32[1]{0:T(128)} %bitcast.1.group, bf16[1024,512]{1,0:T(8,128)(2,1)S(1)} %far_part.3.own, bf16[1024,512]{1,0:T(8,128)(2,1)S(1)} %collective-permute-done.12.peer, ...), custom_call_target="tpu_custom_call" | custom-call | flops 2147483648 | bytes 4194304 | tf_op jit(solution)/shard_map/project/pallas_call | solution.py:310
  57.0 3.6 %collective-permute-done.10.from_up = bf16[512,256]{1,0:T(8,128)(2,1)S(1)} collective-permute-done((bf16[512,256]{1,0:T(8,128)(2,1)S(1)}, bf16[512,256]{1,0:T(8,128)(2,1)S(1)}, u32[]{:S(2)}, u32[]{:S(2)}) %collective-permute-start.10) | collective-permute-done | bytes 262176 | tf_op jit(solution)/shard_map/ppermute | solution.py:360
  60.6 3.4 %collective-permute-done.9.from_down = bf16[512,256]{1,0:T(8,128)(2,1)S(1)} collective-permute-done((bf16[512,256]{1,0:T(8,128)(2,1)S(1)}, bf16[512,256]{1,0:T(8,128)(2,1)S(1)}, u32[]{:S(2)}, u32[]{:S(2)}) %collective-permute-start.9) | collective-permute-done | bytes 262176 | tf_op jit(solution)/shard_map/ppermute | solution.py:360
  64.0 0.1 relay.2
  64.1 0.1 collective-permute-start.13
  64.2 3.2 %collective-permute-start.14 = (bf16[1024,256]{1,0:T(8,128)(2,1)S(1)}, bf16[1024,256]{1,0:T(8,128)(2,1)S(1)}, u32[]{:S(2)}, u32[]{:S(2)}) collective-permute-start(bf16[1024,256]{1,0:T(8,128)(2,1)S(1)} %get-tuple-element.138), channel_id=1, source_target_pairs={{0,6},{1,7},{2,0},{3,1},{4,2},{5,3},{6,4},{7,5},{8,14},{9,15},{10,... | collective-permute-start | bytes 1572872 | tf_op jit(solution)/shard_map/ppermute | solution.py:360
  67.4 3.2 %collective-permute-start.16 = (bf16[512,256]{1,0:T(8,128)(2,1)S(1)}, bf16[512,256]{1,0:T(8,128)(2,1)S(1)}, u32[]{:S(2)}, u32[]{:S(2)}) collective-permute-start(bf16[512,256]{1,0:T(8,128)(2,1)S(1)} %get-tuple-element.142), channel_id=1, source_target_pairs={{0,6},{1,7},{2,0},{3,1},{4,2},{5,3},{6,4},{7,5},{8,14},{9,15},{10,... | collective-permute-start | bytes 786440 | tf_op jit(solution)/shard_map/ppermute | solution.py:360
  70.7 13.3 %collective-permute-done.15.from_down = bf16[512,256]{1,0:T(8,128)(2,1)S(1)} collective-permute-done((bf16[512,256]{1,0:T(8,128)(2,1)S(1)}, bf16[512,256]{1,0:T(8,128)(2,1)S(1)}, u32[]{:S(2)}, u32[]{:S(2)}) %collective-permute-start.15) | collective-permute-done | bytes 262176 | tf_op jit(solution)/shard_map/ppermute | solution.py:360
  83.9 0.1 relay.3
  84.1 0.1 collective-permute-start.17
  84.2 3.2 %collective-permute-start.18 = (bf16[1024,256]{1,0:T(8,128)(2,1)S(1)}, bf16[1024,256]{1,0:T(8,128)(2,1)S(1)}, u32[]{:S(2)}, u32[]{:S(2)}) collective-permute-start(bf16[1024,256]{1,0:T(8,128)(2,1)S(1)} %get-tuple-element.144), channel_id=1, source_target_pairs={{0,6},{1,7},{2,0},{3,1},{4,2},{5,3},{6,4},{7,5},{8,14},{9,15},{10,... | collective-permute-start | bytes 1572872 | tf_op jit(solution)/shard_map/ppermute | solution.py:360
  87.4 0.2 add_convert_fusion.1
  87.6 9.8 %collective-permute-done.17 = bf16[1024,256]{1,0:T(8,128)(2,1)S(1)} collective-permute-done((bf16[1024,256]{1,0:T(8,128)(2,1)S(1)}, bf16[1024,256]{1,0:T(8,128)(2,1)S(1)}, u32[]{:S(2)}, u32[]{:S(2)}) %collective-permute-start.17) | collective-permute-done | bytes 524320 | tf_op jit(solution)/shard_map/ppermute | solution.py:360
  97.4 0.2 add_convert_fusion
  97.6 1.0 %pad_maximum_fusion = bf16[2048,256]{1,0:T(8,128)(2,1)} fusion(bf16[1024,256]{1,0:T(8,128)(2,1)S(1)} %add_convert_fusion, bf16[1024,256]{1,0:T(8,128)(2,1)S(1)} %add_convert_fusion.1), kind=kLoop, calls=%fused_computation | loop fusion | flops 2097152 | bytes 2097152 | tf_op jit(solution)/shard_map/concatenate | solution.py:449
  (17 shorter events, 0.1 us)
Async XLA Ops:
  0.0 2.8 %copy-start.2 = (bf16[2048,3,512]{2,0,1:T(8,128)(2,1)S(1)}, bf16[2048,3,512]{2,0,1:T(8,128)(2,1)}, u32[]{:S(2)}) copy-start(bf16[2048,3,512]{2,0,1:T(8,128)(2,1)} %param.6) | copy-start | bytes 18874372
  2.8 9.1 %copy-start.3 = (bf16[512,2048]{1,0:T(8,128)(2,1)S(1)}, bf16[512,2048]{1,0:T(8,128)(2,1)}, u32[]{:S(2)}) copy-start(bf16[512,2048]{1,0:T(8,128)(2,1)} %w_own.3) | copy-start | bytes 6291460
  10.2 6.7 %collective-permute-start = (bf16[4,128,128]{2,1,0:T(8,128)(2,1)S(1)}, bf16[4,128,128]{2,1,0:T(8,128)(2,1)S(1)}, u32[]{:S(2)}, u32[]{:S(2)}) collective-permute-start(bf16[4,128,128]{2,1,0:T(8,128)(2,1)S(1)} %get-tuple-element.79.refs_0_), channel_id=1, source_target_pairs={{0,8},{8,0},{16,24},{24,16},{32,40},{40,32},{48,56},{56,48},{64,72... | collective-permute-start | bytes 393224 | tf_op jit(solution)/shard_map/ppermute | solution.py:373
  11.9 34.6 %collective-permute-start.8 = (bf16[512,2048]{1,0:T(8,128)(2,1)S(1)}, bf16[512,2048]{1,0:T(8,128)(2,1)S(1)}, u32[]{:S(2)}, u32[]{:S(2)}) collective-permute-start(bf16[512,2048]{1,0:T(8,128)(2,1)S(1)} %copy-done.3), channel_id=1, source_target_pairs={{0,1},{1,0},{2,3},{3,2},{4,5},{5,4},{6,7},{7,6},{8,9},{9,8},{10,11... | collective-permute-start | bytes 6291464 | tf_op jit(solution)/shard_map/ppermute | solution.py:357
  11.9 7.9 %copy-start = (bf16[4,128,17]{1,0,2:T(4,128)(2,1)S(1)}, bf16[4,128,17]{1,0,2:T(4,128)(2,1)}, u32[]{:S(2)}) copy-start(bf16[4,128,17]{1,0,2:T(4,128)(2,1)} %param.7) | copy-start | bytes 52228
  17.0 7.2 %collective-permute-start.1 = (bf16[4,128,128]{2,1,0:T(8,128)(2,1)S(1)}, bf16[4,128,128]{2,1,0:T(8,128)(2,1)S(1)}, u32[]{:S(2)}, u32[]{:S(2)}) collective-permute-start(bf16[4,128,128]{2,1,0:T(8,128)(2,1)S(1)} %added.4.after.refs_0_), channel_id=1, source_target_pairs={{0,24},{8,16},{16,8},{24,0},{32,56},{40,48},{48,40},{56,32},{64,88... | collective-permute-start | bytes 393224 | tf_op jit(solution)/shard_map/ppermute | solution.py:373
  19.2 5.6 %collective-permute-start.2 = (bf16[4,128,128]{2,1,0:T(8,128)(2,1)S(1)}, bf16[4,128,128]{2,1,0:T(8,128)(2,1)S(1)}, u32[]{:S(2)}, u32[]{:S(2)}) collective-permute-start(bf16[4,128,128]{2,1,0:T(8,128)(2,1)S(1)} %get-tuple-element.85.refs_2_), channel_id=1, source_target_pairs={{0,8},{8,0},{16,24},{24,16},{32,40},{40,32},{48,56},{56,48},{64,72... | collective-permute-start | bytes 393224 | tf_op jit(solution)/shard_map/ppermute | solution.py:373
  24.9 6.4 %collective-permute-start.3 = (bf16[4,128,128]{2,1,0:T(8,128)(2,1)S(1)}, bf16[4,128,128]{2,1,0:T(8,128)(2,1)S(1)}, u32[]{:S(2)}, u32[]{:S(2)}) collective-permute-start(bf16[4,128,128]{2,1,0:T(8,128)(2,1)S(1)} %get-tuple-element.97.after.refs_0_), channel_id=1, source_target_pairs={{0,32},{8,40},{16,48},{24,56},{32,0},{40,8},{48,16},{56,24},{64,96... | collective-permute-start | bytes 393224 | tf_op jit(solution)/shard_map/ppermute | solution.py:373
  26.9 6.2 %collective-permute-start.4 = (bf16[4,128,128]{2,1,0:T(8,128)(2,1)S(1)}, bf16[4,128,128]{2,1,0:T(8,128)(2,1)S(1)}, u32[]{:S(2)}, u32[]{:S(2)}) collective-permute-start(bf16[4,128,128]{2,1,0:T(8,128)(2,1)S(1)} %get-tuple-element.98.refs_2_), channel_id=1, source_target_pairs={{0,24},{8,16},{16,8},{24,0},{32,56},{40,48},{48,40},{56,32},{64,88... | collective-permute-start | bytes 393224 | tf_op jit(solution)/shard_map/ppermute | solution.py:373
  33.1 6.4 %collective-permute-start.5 = (bf16[4,128,128]{2,1,0:T(8,128)(2,1)S(1)}, bf16[4,128,128]{2,1,0:T(8,128)(2,1)S(1)}, u32[]{:S(2)}, u32[]{:S(2)}) collective-permute-start(bf16[4,128,128]{2,1,0:T(8,128)(2,1)S(1)} %get-tuple-element.106.after.refs_0_), channel_id=1, source_target_pairs={{0,96},{8,104},{16,112},{24,120},{32,64},{40,72},{48,80},{56,88},{... | collective-permute-start | bytes 393224 | tf_op jit(solution)/shard_map/ppermute | solution.py:373
  35.8 5.0 %collective-permute-start.6 = (bf16[4,128,128]{2,1,0:T(8,128)(2,1)S(1)}, bf16[4,128,128]{2,1,0:T(8,128)(2,1)S(1)}, u32[]{:S(2)}, u32[]{:S(2)}) collective-permute-start(bf16[4,128,128]{2,1,0:T(8,128)(2,1)S(1)} %get-tuple-element.107.refs_2_), channel_id=1, source_target_pairs={{0,32},{8,40},{16,48},{24,56},{32,0},{40,8},{48,16},{56,24},{64,96... | collective-permute-start | bytes 393224 | tf_op jit(solution)/shard_map/ppermute | solution.py:373
  36.8 4.0 %copy-start.1 = (f32[512]{0:T(512)S(1)}, f32[512]{0:T(512)}, u32[]{:S(2)}) copy-start(f32[512]{0:T(512)} %param.8) | copy-start | bytes 6148
  42.3 4.3 %collective-permute-start.7 = (bf16[1024,512]{1,0:T(8,128)(2,1)S(1)}, bf16[1024,512]{1,0:T(8,128)(2,1)S(1)}, u32[]{:S(2)}, u32[]{:S(2)}) collective-permute-start(bf16[1024,512]{1,0:T(8,128)(2,1)S(1)} %far_part.2.own.after), channel_id=1, source_target_pairs={{0,1},{1,0},{2,3},{3,2},{4,5},{5,4},{6,7},{7,6},{8,9},{9,8},{10,11... | collective-permute-start | bytes 3145736 | tf_op jit(solution)/shard_map/ppermute | solution.py:357
  42.4 7.1 %collective-permute-start.11 = (bf16[4,128,128]{2,1,0:T(8,128)(2,1)S(1)}, bf16[4,128,128]{2,1,0:T(8,128)(2,1)S(1)}, u32[]{:S(2)}, u32[]{:S(2)}) collective-permute-start(bf16[4,128,128]{2,1,0:T(8,128)(2,1)S(1)} %get-tuple-element.135), channel_id=1, source_target_pairs={{0,96},{8,104},{16,112},{24,120},{32,64},{40,72},{48,80},{56,88},{... | collective-permute-start | bytes 393224 | tf_op jit(solution)/shard_map/ppermute | solution.py:373
  51.2 3.4 %collective-permute-start.12 = (bf16[1024,512]{1,0:T(8,128)(2,1)S(1)}, bf16[1024,512]{1,0:T(8,128)(2,1)S(1)}, u32[]{:S(2)}, u32[]{:S(2)}) collective-permute-start(bf16[1024,512]{1,0:T(8,128)(2,1)S(1)} %far_part.3.own), channel_id=1, source_target_pairs={{0,1},{1,0},{2,3},{3,2},{4,5},{5,4},{6,7},{7,6},{8,9},{9,8},{10,11... | collective-permute-start | bytes 3145736 | tf_op jit(solution)/shard_map/ppermute | solution.py:357
  51.3 9.2 %collective-permute-start.10 = (bf16[512,256]{1,0:T(8,128)(2,1)S(1)}, bf16[512,256]{1,0:T(8,128)(2,1)S(1)}, u32[]{:S(2)}, u32[]{:S(2)}) collective-permute-start(bf16[512,256]{1,0:T(8,128)(2,1)S(1)} %get-tuple-element.128), channel_id=1, source_target_pairs={{0,6},{1,7},{2,0},{3,1},{4,2},{5,3},{6,4},{7,5},{8,14},{9,15},{10,... | collective-permute-start | bytes 786440 | tf_op jit(solution)/shard_map/ppermute | solution.py:360
  54.6 9.3 %collective-permute-start.9 = (bf16[512,256]{1,0:T(8,128)(2,1)S(1)}, bf16[512,256]{1,0:T(8,128)(2,1)S(1)}, u32[]{:S(2)}, u32[]{:S(2)}) collective-permute-start(bf16[512,256]{1,0:T(8,128)(2,1)S(1)} %get-tuple-element.127.after), channel_id=1, source_target_pairs={{0,2},{1,3},{2,4},{3,5},{4,6},{5,7},{6,0},{7,1},{8,10},{9,11},{10,... | collective-permute-start | bytes 786440 | tf_op jit(solution)/shard_map/ppermute | solution.py:360
  64.1 23.3 %collective-permute-start.13 = (bf16[1024,256]{1,0:T(8,128)(2,1)S(1)}, bf16[1024,256]{1,0:T(8,128)(2,1)S(1)}, u32[]{:S(2)}, u32[]{:S(2)}) collective-permute-start(bf16[1024,256]{1,0:T(8,128)(2,1)S(1)} %get-tuple-element.137), channel_id=1, source_target_pairs={{0,2},{1,3},{2,4},{3,5},{4,6},{5,7},{6,0},{7,1},{8,10},{9,11},{10,... | collective-permute-start | bytes 1572872 | tf_op jit(solution)/shard_map/ppermute | solution.py:360
  64.2 23.2 %collective-permute-start.14 = (bf16[1024,256]{1,0:T(8,128)(2,1)S(1)}, bf16[1024,256]{1,0:T(8,128)(2,1)S(1)}, u32[]{:S(2)}, u32[]{:S(2)}) collective-permute-start(bf16[1024,256]{1,0:T(8,128)(2,1)S(1)} %get-tuple-element.138), channel_id=1, source_target_pairs={{0,6},{1,7},{2,0},{3,1},{4,2},{5,3},{6,4},{7,5},{8,14},{9,15},{10,... | collective-permute-start | bytes 1572872 | tf_op jit(solution)/shard_map/ppermute | solution.py:360
  67.4 16.5 %collective-permute-start.15 = (bf16[512,256]{1,0:T(8,128)(2,1)S(1)}, bf16[512,256]{1,0:T(8,128)(2,1)S(1)}, u32[]{:S(2)}, u32[]{:S(2)}) collective-permute-start(bf16[512,256]{1,0:T(8,128)(2,1)S(1)} %get-tuple-element.136.after), channel_id=1, source_target_pairs={{0,2},{1,3},{2,4},{3,5},{4,6},{5,7},{6,0},{7,1},{8,10},{9,11},{10,... | collective-permute-start | bytes 786440 | tf_op jit(solution)/shard_map/ppermute | solution.py:360
  67.4 16.5 %collective-permute-start.16 = (bf16[512,256]{1,0:T(8,128)(2,1)S(1)}, bf16[512,256]{1,0:T(8,128)(2,1)S(1)}, u32[]{:S(2)}, u32[]{:S(2)}) collective-permute-start(bf16[512,256]{1,0:T(8,128)(2,1)S(1)} %get-tuple-element.142), channel_id=1, source_target_pairs={{0,6},{1,7},{2,0},{3,1},{4,2},{5,3},{6,4},{7,5},{8,14},{9,15},{10,... | collective-permute-start | bytes 786440 | tf_op jit(solution)/shard_map/ppermute | solution.py:360
  84.1 13.3 %collective-permute-start.17 = (bf16[1024,256]{1,0:T(8,128)(2,1)S(1)}, bf16[1024,256]{1,0:T(8,128)(2,1)S(1)}, u32[]{:S(2)}, u32[]{:S(2)}) collective-permute-start(bf16[1024,256]{1,0:T(8,128)(2,1)S(1)} %get-tuple-element.143), channel_id=1, source_target_pairs={{0,2},{1,3},{2,4},{3,5},{4,6},{5,7},{6,0},{7,1},{8,10},{9,11},{10,... | collective-permute-start | bytes 1572872 | tf_op jit(solution)/shard_map/ppermute | solution.py:360
  84.2 13.2 %collective-permute-start.18 = (bf16[1024,256]{1,0:T(8,128)(2,1)S(1)}, bf16[1024,256]{1,0:T(8,128)(2,1)S(1)}, u32[]{:S(2)}, u32[]{:S(2)}) collective-permute-start(bf16[1024,256]{1,0:T(8,128)(2,1)S(1)} %get-tuple-element.144), channel_id=1, source_target_pairs={{0,6},{1,7},{2,0},{3,1},{4,2},{5,3},{6,4},{7,5},{8,14},{9,15},{10,... | collective-permute-start | bytes 1572872 | tf_op jit(solution)/shard_map/ppermute | solution.py:360
where the time goes:
time: 98.8 us; the launch traced here: 98.7 us
  waiting for transfers between devices  36 us (36%)
  Pallas kernels  32.1 us (32%)
  starting transfers between devices  26.2 us (27%)
  local copies, waits for them, and re-layouts  2.8 us (3%)
  other arithmetic  1.45 us (1%)
    ppermute x8, waiting for transfers between devices, over_ring(): lax.ppermute(value, 'head', [(i, (i + 2 * shift) % head_count) for i in r...  30.1 us
    ppermute x8, starting transfers between devices, over_ring(): lax.ppermute(value, 'head', [(i, (i + 2 * shift) % head_count) for i in r...  13.1 us
    ppermute x8, starting transfers between devices, over_ctx(): return lax.ppermute(value, 'ctx', [(i, i ^ mask) for i in range(ctx_count)])  12.9 us
    pallas_call x2, Pallas kernels, key_value(): pl.pallas_call(functools.partial(first_kernel if first else second_kernel...  12.5 us
    pallas_call x4, Pallas kernels, near_part(): pl.pallas_call(functools.partial(near_kernel, heads, dim, half, step), in...  11.2 us
    ppermute x8, waiting for transfers between devices, over_ctx(): return lax.ppermute(value, 'ctx', [(i, i ^ mask) for i in range(ctx_count)])  5.9 us
    pallas_call x2, Pallas kernels, project(): pl.pallas_call(functools.partial(project_kernel, feats, ring), in_specs=[...  4.72 us
    pallas_call x2, Pallas kernels, far_part(): pl.pallas_call(functools.partial(far_kernel, heads, dim, level0, count, c...  3.23 us
  transfers between devices with their start and end apart: 19, of which 9 were waited for; matrix products, arithmetic and copies ran while one was open for 0% of the time, Pallas kernels for 23%

commit v1 on v0

--- a/solution.py
+++ b/solution.py
@@ -63,8 +63,10 @@
         pairs.append((w_in.at[1, at], wk.at[at]))
         pairs.append((tok_in.at[head_rows, at], tok.at[head_rows, at]))
     pairs.append((w_in.at[2], wv))
-    rest = pl.ds(BLOCK, tok.shape[0] - BLOCK)
-    pairs.append((tok_in.at[rest], tok.at[rest]))
+    rows = k_out.shape[0]
+    for start, stop in ((BLOCK, rows), (rows, tok.shape[0])):
+        at = pl.ds(start, stop - start)
+        pairs.append((tok_in.at[at], tok.at[at]))
     pairs.append((w_in.at[0], wq))
     copies = [pltpu.make_async_copy(*pair, sems.at[j]) for j, pair in enumerate(pairs)]
     for copy in copies[:4]:
@@ -73,18 +75,20 @@
     for j in range(2):
         copies[2 * j].wait()
         copies[2 * j + 1].wait()
-        for copy in copies[4 + j : 5 + 2 * j]:
-            copy.start()
+        copies[4 + j].start()
         at = slice(j * part, (j + 1) * part)
         term = dot(tok[:BLOCK, at], wk[at])
         keys = term if keys is None else keys + term
     copies[4].wait()
+    copies[6].start()
+    copies[7].start()
     outs = (wk, wv, k_out, vt_out, chunk_out, total)
     key_value_block(heads, dim, 0, tok[:BLOCK], *outs, keys)
     copies[5].wait()
     for block in range(1, blocks):
         key_value_block(heads, dim, block, tok[block * BLOCK : (block + 1) * BLOCK], *outs)
     copies[6].wait()
+    copies[7].wait()
     total_out[...] = total[...].astype(BF16)
 
 
@@ -110,7 +114,7 @@
     if first:
         shapes.append(jax.ShapeDtypeStruct(args[0].shape, BF16))
         shapes += [jax.ShapeDtypeStruct((depth, width), BF16)] * 3
-        scratch.append(pltpu.SemaphoreType.DMA((7,)))
+        scratch.append(pltpu.SemaphoreType.DMA((8,)))
     return pl.pallas_call(
         functools.partial(first_kernel if first else second_kernel, heads, dim),
         in_specs=[pl.BlockSpec(memory_space=pltpu.HBM)] * 2 if first else [vmem] * 3,
@@ -289,7 +293,7 @@
     )(device, after, gain, *blocks, *states)
 
 
-def project_kernel(feats, ring, group, own, peer, w_own, w_peer, top, bottom, up, down, mine):
+def project_kernel(feats, ring, group, own, peer, w_own, w_peer, *outs):
     block = own.shape[0] // 2
     for order, shift in enumerate((2, 1, ring - 1, 0)):
         slot = 2 * (((group[0] >> 1) + shift) % ring) + (group[0] & 1)
@@ -297,49 +301,83 @@
         for part in range(2):
             rows = slice(part * block, (part + 1) * block)
             total = dot(own[rows], w_own[:, at]) + dot(peer[rows], w_peer[:, at])
-            if order == 0:
-                (top, bottom)[part][...] = total.astype(BF16)
-            else:
-                out = (up, down, mine)[order - 1]
-                out[rows] = total.astype(out.dtype)
+            out = outs[2 * order + part]
+            out[...] = total.astype(out.dtype)
 
 
 def project(group, ring, own, peer, w_own, w_peer, feats):
     rows, width = own.shape
     vmem = pl.BlockSpec(memory_space=pltpu.VMEM)
+    size = (rows // 2, feats)
     return pl.pallas_call(
         functools.partial(project_kernel, feats, ring),
         in_specs=[pl.BlockSpec(memory_space=pltpu.SMEM)] + [vmem] * 4,
-        out_specs=[vmem] * 5,
-        out_shape=[jax.ShapeDtypeStruct((rows // 2, feats), BF16)] * 2
-        + [jax.ShapeDtypeStruct((rows, feats), BF16)] * 2
-        + [jax.ShapeDtypeStruct((rows, feats), F32)],
+        out_specs=[vmem] * 8,
+        out_shape=[jax.ShapeDtypeStruct(size, BF16)] * 6 + [jax.ShapeDtypeStruct(size, F32)] * 2,
         compiler_params=pltpu.CompilerParams(vmem_limit_bytes=12 << 20),
         cost_estimate=cost(16 * rows * width * feats, 4),
         name="project",
     )(group, own, peer, w_own, w_peer)
 
 
-def relay_kernel(up_in, down_in, from_down, from_up, after, up, down):
-    del after
+def relay_kernel(up_in, down_in, from_down, from_up, *refs):
+    up, down = refs[-2:]
     block = from_down.shape[0]
-    up[:block] = (up_in[:block].astype(F32) + from_down[...].astype(F32)).astype(BF16)
-    up[block:] = up_in[block:]
-    down[:block] = down_in[:block]
-    down[block:] = (down_in[block:].astype(F32) + from_up[...].astype(F32)).astype(BF16)
-
-
-def relay(up, down, from_down, from_up, after):
-    vmem = pl.BlockSpec(memory_space=pltpu.VMEM)
+    up[:block] = (up_in[...].astype(F32) + from_down[...].astype(F32)).astype(BF16)
+    down[:block] = (down_in[...].astype(F32) + from_up[...].astype(F32)).astype(BF16)
+    for extra, out in zip(refs[:-2], (up, down)):
+        out[block:] = extra[...]
+
+
+def relay(up, down, from_down, from_up, *extra):
+    rows, feats = up.shape
+    vmem = pl.BlockSpec(memory_space=pltpu.VMEM)
+    total = 2 * rows if extra else rows
     return pl.pallas_call(
         relay_kernel,
-        in_specs=[vmem] * 4 + [pl.BlockSpec(memory_space=pl.ANY)],
+        in_specs=[vmem] * (4 + len(extra)),
         out_specs=[vmem] * 2,
-        out_shape=[jax.ShapeDtypeStruct(up.shape, BF16)] * 2,
+        out_shape=[jax.ShapeDtypeStruct((total, feats), BF16)] * 2,
         compiler_params=pltpu.CompilerParams(vmem_limit_bytes=SMALL << 20),
         cost_estimate=cost(1 << 18, 1),
         name="relay",
-    )(up, down, from_down, from_up, after)
+    )(up, down, from_down, from_up, *extra)
+
+
+def final_kernel(half, parts, *refs):
+    out, stage, sems = refs[-3:]
+    block = stage.shape[1]
+    copies = []
+    for part in range(2):
+        own, first, second = refs[3 * part : 3 * part + 3]
+        (at1, at2) = parts[part]
+        total = own[...] + first[at1 : at1 + block].astype(F32) + second[at2 : at2 + block].astype(F32)
+        stage[part] = total.astype(BF16)
+        rows = pl.ds((2 * half + part) * block, block)
+        copies.append(pltpu.make_async_copy(stage.at[part], out.at[rows], sems.at[part]))
+        copies[-1].start()
+    for copy in copies:
+        copy.wait()
+
+
+def final(half, terms, parts, base):
+    block, feats = terms[0].shape
+    vmem = pl.BlockSpec(memory_space=pltpu.VMEM)
+    hbm = pl.BlockSpec(memory_space=pltpu.HBM)
+    args, specs, alias = list(terms), [vmem] * 6, {}
+    if base is not None:
+        args, specs, alias = args + [base], specs + [hbm], {6: 0}
+    return pl.pallas_call(
+        functools.partial(final_kernel, half, parts),
+        in_specs=specs,
+        out_specs=hbm,
+        out_shape=jax.ShapeDtypeStruct((4 * block, feats), BF16),
+        scratch_shapes=[pltpu.VMEM((2, block, feats), BF16), pltpu.SemaphoreType.DMA((2,))],
+        input_output_aliases=alias,
+        compiler_params=pltpu.CompilerParams(vmem_limit_bytes=SMALL << 20),
+        cost_estimate=cost(1 << 18, 2),
+        name="final",
+    )(*args)
 
 
 def shards(tokens, project_weight, level_weight, norm_gain, output_weight):
@@ -372,6 +410,8 @@
     def over_ctx(value, mask):
         return lax.ppermute(value, "ctx", [(i, i ^ mask) for i in range(ctx_count)])
 
+    weights = pltpu.with_memory_space_constraint(weights, pltpu.HBM)
+    tokens = pltpu.with_memory_space_constraint(tokens, pltpu.HBM)
     low = key_value(heads, dim, half_rows, (tokens, weights), True)
     rows, weight_q, weight_k, weight_v = low[4:]
     held = [None, None]
@@ -420,9 +460,6 @@
     levels_of[1].append(high_z3)
     levels_of[1].append(sums[0])
 
-    def joined(*terms):
-        return functools.reduce(jnp.add, [term.astype(F32) for term in terms]).astype(BF16)
-
     def attended(half, after):
         parts = [near[half, 0], near[half, 1]]
         return far_part(where_ctx, after, parts, gain, levels_of[half], heads, dim, level0)
@@ -430,23 +467,28 @@
     def sent(own, peer):
         return project(where_head, ring, own, peer, output_weight, peer_weight, feats)
 
+    def sent_over(value, shift):
+        return over_ring(value, shift)
+
     own_low = attended(0, sums[0])
     peer_low = over_core(own_low)
     near[1, 1] = near_part(held[1], own_low, 1, 1, heads, dim)
-    sends = [sent(own_low, peer_low)]
-    own_high = attended(1, sends[0][0])
-    sends.append(sent(own_high, over_core(own_high)))
-    results = []
-
-    low_pair = [over_ring(sends[0][0], 1), over_ring(sends[0][1], -1)]
-    high_pair = [over_ring(sends[1][0], 1), over_ring(sends[1][1], -1)]
-    arrived = [low_pair, high_pair]
-    for half in range(2):
-        up, down, mine = sends[half][2:]
-        make = lambda: relay(up, down, *arrived[half], sends[1][0])
-        up, down = make()
-        results.append(joined(mine, over_ring(up, 1), over_ring(down, -1)))
-    return jnp.concatenate(results, axis=0)
+    top, bottom, up_a, up_b, down_a, down_b, low_a, low_b = sent(own_low, peer_low)
+    low_pair = [sent_over(top, 1), sent_over(bottom, -1)]
+    own_high = attended(1, top)
+    low_up_b, low_down_a = sent_over(up_b, 1), sent_over(down_a, -1)
+    peer_high = over_core(own_high)
+    top, bottom, high_up_a, high_up_b, high_down_a, high_down_b, high_a, high_b = sent(own_high, peer_high)
+    high_pair = [sent_over(top, 1), sent_over(bottom, -1)]
+    up_mix, down_mix = relay(up_a, down_b, *low_pair, high_up_b, high_down_a)
+    up_mix, down_mix = sent_over(up_mix, 1), sent_over(down_mix, -1)
+    up_last, down_last = relay(high_up_a, high_down_b, *high_pair)
+    up_last, down_last = over_ring(up_last, 1), over_ring(down_last, -1)
+    block = half_rows // 2
+    low_terms = (low_a, up_mix, low_down_a, low_b, low_up_b, down_mix)
+    result = final(0, low_terms, ((0, 0), (0, 0)), None)
+    high_terms = (high_a, up_last, down_mix, high_b, up_mix, down_last)
+    return final(1, high_terms, ((0, block), (block, 0)), result)
 
 
 def solution(mesh):

time: 98.8 us -> 91 us (0.921)
  waiting for transfers between devices: 36 us -> 25.5 us
  starting transfers between devices: 26.2 us -> 30 us
  local copies, waits for them, and re-layouts: 2.8 us -> 0.01 us
  Pallas kernels: 32.1 us -> 34.3 us
  other arithmetic: 1.45 us -> 0 us
    ppermute x8 -> x10, waiting for transfers between devices: 30.1 us -> 19.7 us  [over_ring(): lax.ppermute(value, 'head', [(i, (i + 2 * shift) % head_count) for i in r...]
    ppermute x8 -> x10, starting transfers between devices: 13.1 us -> 17 us  [over_ring(): lax.ppermute(value, 'head', [(i, (i + 2 * shift) % head_count) for i in r...]
    unnamed x8 -> x6, local copies, waits for them, and re-layouts: 2.8 us -> 0.01 us
    pallas_call x2 -> x4, Pallas kernels: 0.27 us -> 2.06 us  [the longest x2 1.8 us: final(): pl.pallas_call(functools.partial(final_kernel, half, parts), in_specs=spe...]
    concatenate x1 -> x0, other arithmetic: 1.04 us -> none  [shards(): return jnp.concatenate(results, axis=0)]
  transfers between devices with their start and end apart: 19 -> 21, of which waited for: 9 -> 10; matrix products, arithmetic and copies ran while one was open for 0% -> 0% of each run, Pallas kernels for 23% -> 26%
where the time goes in v1:
time: 91 us; the launch traced here: 90.3 us
  Pallas kernels  34.3 us (38%)
  starting transfers between devices  30 us (33%)
  waiting for transfers between devices  25.5 us (28%)
    ppermute x10, waiting for transfers between devices, over_ring(): lax.ppermute(value, 'head', [(i, (i + 2 * shift) % head_count) for i in r...  19.7 us
    ppermute x10, starting transfers between devices, over_ring(): lax.ppermute(value, 'head', [(i, (i + 2 * shift) % head_count) for i in r...  17 us
    pallas_call x2, Pallas kernels, key_value(): pl.pallas_call(functools.partial(first_kernel if first else second_kernel...  12.9 us
    ppermute x8, starting transfers between devices, over_ctx(): return lax.ppermute(value, 'ctx', [(i, i ^ mask) for i in range(ctx_count)])  12.9 us
    pallas_call x4, Pallas kernels, near_part(): pl.pallas_call(functools.partial(near_kernel, heads, dim, half, step), in...  11.2 us
    ppermute x8, waiting for transfers between devices, over_ctx(): return lax.ppermute(value, 'ctx', [(i, i ^ mask) for i in range(ctx_count)])  5.88 us
    pallas_call x2, Pallas kernels, project(): pl.pallas_call(functools.partial(project_kernel, feats, ring), in_specs=[...  4.71 us
    pallas_call x2, Pallas kernels, far_part(): pl.pallas_call(functools.partial(far_kernel, heads, dim, level0, count, c...  3.23 us
  transfers between devices with their start and end apart: 21, of which 10 were waited for; matrix products, arithmetic and copies ran while one was open for 0% of the time, Pallas kernels for 26%

profile of v1, /device:TPU:0, one launch (start us, length us, event | category | flops | bytes accessed | tf_op | source)
XLA Modules:
  0.0 90.3 jit_solution(8965044351466919027)
XLA Ops:
  0.0 7.9 %key_value.2 = (bf16[1024,512]{1,0:T(8,128)(2,1)S(1)}, bf16[2,512,512]{2,1,0:T(8,128)(2,1)S(1)}, bf16[4,4,128,128]{3,2,1,0:T(8,128)(2,1)S(1)}, bf16[4,128,128]{2...) custom-call(bf16[2048,2048]{1,0:T(8,128)(2,1)} %tok_in, ...), custom_call_target="tpu_custom_call" | custom-call | flops 4294967296 | bytes 14680064 | tf_op jit(solution)/shard_map/key_value/pallas_call | solution.py:118
  7.9 1.7 %collective-permute-start = (bf16[4,128,128]{2,1,0:T(8,128)(2,1)S(1)}, bf16[4,128,128]{2,1,0:T(8,128)(2,1)S(1)}, u32[]{:S(2)}, u32[]{:S(2)}) collective-permute-start(bf16[4,128,128]{2,1,0:T(8,128)(2,1)S(1)} %get-tuple-element.85.refs_0_), channel_id=1, source_target_pairs={{0,8},{8,0},{16,24},{24,16},{32,40},{40,32},{48,56},{56,48},{64,72... | collective-permute-start | bytes 393224 | tf_op jit(solution)/shard_map/ppermute | solution.py:411
  9.6 0.0 collective-permute-start.8
  9.6 5.0 %key_value.3 = (bf16[1024,512]{1,0:T(8,128)(2,1)S(1)}, bf16[2,512,512]{2,1,0:T(8,128)(2,1)S(1)}, bf16[4,4,128,128]{3,2,1,0:T(8,128)(2,1)S(1)}, bf16[4,128,128]{2,1,0:T(8,128)(2,1)S(1)}) custom-call(bf16[2048,2048]{1,0:T(8,128)(2,1)S(1)} %get-tuple-element.114.tok, bf16[2048,512]{1,0:T(8,128)(2,1)S(1)} %get-tuple-element.86.wk, ...), custom_call_target="tpu_custom_call" | custom-call | flops 4294967296 | bytes 14680064 | tf_op jit(solution)/shard_map/key_value/pallas_call | solution.py:118
  14.7 2.2 %collective-permute-start.1 = (bf16[4,128,128]{2,1,0:T(8,128)(2,1)S(1)}, bf16[4,128,128]{2,1,0:T(8,128)(2,1)S(1)}, u32[]{:S(2)}, u32[]{:S(2)}) collective-permute-start(bf16[4,128,128]{2,1,0:T(8,128)(2,1)S(1)} %added.4.after.refs_0_), channel_id=1, source_target_pairs={{0,24},{8,16},{16,8},{24,0},{32,56},{40,48},{48,40},{56,32},{64,88... | collective-permute-start | bytes 393224 | tf_op jit(solution)/shard_map/ppermute | solution.py:411
  16.9 0.6 collective-permute-start.2
  17.5 2.7 %near_part.4 = (f32[512,512]{1,0:T(8,128)S(1)}, bf16[512,512]{1,0:T(8,128)(2,1)S(1)}, f32[68,512]{1,0:T(8,128)S(1)}) custom-call(bf16[2048,2048]{1,0:T(8,128)(2,1)S(1)} %get-tuple-element.114.tok, bf16[2048,512]{1,0:T(8,128)(2,1)S(1)} %get-tuple-element.93.wq, bf16[1024,512]{1,0:T(8,128)(2,1)S(1)} %get-tuple-element.94.keys, ...), custom_call_target="tpu_custom_call" | custom-call | flops 2147483648 | bytes 14680064 | tf_op jit(solution)/shard_map/near_part/pallas_call | solution.py:230
  20.2 1.7 %collective-permute-done.1.refs_1_.refs_7_ = bf16[4,128,128]{2,1,0:T(8,128)(2,1)S(1)} collective-permute-done((bf16[4,128,128]{2,1,0:T(8,128)(2,1)S(1)}, bf16[4,128,128]{2,1,0:T(8,128)(2,1)S(1)}, u32[]{:S(2)}, u32[]{:S(2)}) %collective-permute-start.1) | collective-permute-done | bytes 131104 | tf_op jit(solution)/shard_map/ppermute | solution.py:411
  21.9 0.6 collective-permute-done.2.refs_3_.refs_6_
  22.5 0.1 added.5
  22.6 2.0 %collective-permute-start.3 = (bf16[4,128,128]{2,1,0:T(8,128)(2,1)S(1)}, bf16[4,128,128]{2,1,0:T(8,128)(2,1)S(1)}, u32[]{:S(2)}, u32[]{:S(2)}) collective-permute-start(bf16[4,128,128]{2,1,0:T(8,128)(2,1)S(1)} %get-tuple-element.103.after.refs_0_), channel_id=1, source_target_pairs={{0,32},{8,40},{16,48},{24,56},{32,0},{40,8},{48,16},{56,24},{64,96... | collective-permute-start | bytes 393224 | tf_op jit(solution)/shard_map/ppermute | solution.py:411
  24.6 1.5 %collective-permute-start.4 = (bf16[4,128,128]{2,1,0:T(8,128)(2,1)S(1)}, bf16[4,128,128]{2,1,0:T(8,128)(2,1)S(1)}, u32[]{:S(2)}, u32[]{:S(2)}) collective-permute-start(bf16[4,128,128]{2,1,0:T(8,128)(2,1)S(1)} %get-tuple-element.104.refs_2_), channel_id=1, source_target_pairs={{0,24},{8,16},{16,8},{24,0},{32,56},{40,48},{48,40},{56,32},{64,88... | collective-permute-start | bytes 393224 | tf_op jit(solution)/shard_map/ppermute | solution.py:411
  26.1 2.9 %near_part.5 = (f32[512,512]{1,0:T(8,128)S(1)}, bf16[512,512]{1,0:T(8,128)(2,1)S(1)}, f32[68,512]{1,0:T(8,128)S(1)}) custom-call(bf16[2048,2048]{1,0:T(8,128)(2,1)S(1)} %get-tuple-element.114.tok, bf16[2048,512]{1,0:T(8,128)(2,1)S(1)} %get-tuple-element.93.wq, bf16[1024,512]{1,0:T(8,128)(2,1)S(1)} %get-tuple-element.94.keys, ...), custom_call_target="tpu_custom_call" | custom-call | flops 2147483648 | bytes 14680064 | tf_op jit(solution)/shard_map/near_part/pallas_call | solution.py:230
  28.9 0.0 collective-permute-done.3.refs_1_.refs_8_
  28.9 1.8 %collective-permute-done.4.refs_3_.refs_7_ = bf16[4,128,128]{2,1,0:T(8,128)(2,1)S(1)} collective-permute-done((bf16[4,128,128]{2,1,0:T(8,128)(2,1)S(1)}, bf16[4,128,128]{2,1,0:T(8,128)(2,1)S(1)}, u32[]{:S(2)}, u32[]{:S(2)}) %collective-permute-start.4) | collective-permute-done | bytes 131104 | tf_op jit(solution)/shard_map/ppermute | solution.py:411
  30.7 0.1 added.6
  30.8 2.6 %collective-permute-start.5 = (bf16[4,128,128]{2,1,0:T(8,128)(2,1)S(1)}, bf16[4,128,128]{2,1,0:T(8,128)(2,1)S(1)}, u32[]{:S(2)}, u32[]{:S(2)}) collective-permute-start(bf16[4,128,128]{2,1,0:T(8,128)(2,1)S(1)} %get-tuple-element.112.after.refs_0_), channel_id=1, source_target_pairs={{0,96},{8,104},{16,112},{24,120},{32,64},{40,72},{48,80},{56,88},{... | collective-permute-start | bytes 393224 | tf_op jit(solution)/shard_map/ppermute | solution.py:411
  33.4 1.0 %collective-permute-start.6 = (bf16[4,128,128]{2,1,0:T(8,128)(2,1)S(1)}, bf16[4,128,128]{2,1,0:T(8,128)(2,1)S(1)}, u32[]{:S(2)}, u32[]{:S(2)}) collective-permute-start(bf16[4,128,128]{2,1,0:T(8,128)(2,1)S(1)} %get-tuple-element.113.refs_2_), channel_id=1, source_target_pairs={{0,32},{8,40},{16,48},{24,56},{32,0},{40,8},{48,16},{56,24},{64,96... | collective-permute-start | bytes 393224 | tf_op jit(solution)/shard_map/ppermute | solution.py:411
  34.4 2.7 %near_part.6 = (f32[512,512]{1,0:T(8,128)S(1)}, bf16[512,512]{1,0:T(8,128)(2,1)S(1)}, f32[68,512]{1,0:T(8,128)S(1)}) custom-call(bf16[2048,2048]{1,0:T(8,128)(2,1)S(1)} %get-tuple-element.114.tok, bf16[2048,512]{1,0:T(8,128)(2,1)S(1)} %get-tuple-element.93.wq, bf16[1024,512]{1,0:T(8,128)(2,1)S(1)} %get-tuple-element.115.keys, ...), custom_call_target="tpu_custom_call" | custom-call | flops 2147483648 | bytes 14680064 | tf_op jit(solution)/shard_map/near_part/pallas_call | solution.py:230
  37.2 0.0 collective-permute-done.5.refs_1_.refs_9_
  37.2 1.2 %collective-permute-done.6.refs_3_.refs_8_ = bf16[4,128,128]{2,1,0:T(8,128)(2,1)S(1)} collective-permute-done((bf16[4,128,128]{2,1,0:T(8,128)(2,1)S(1)}, bf16[4,128,128]{2,1,0:T(8,128)(2,1)S(1)}, u32[]{:S(2)}, u32[]{:S(2)}) %collective-permute-start.6) | collective-permute-done | bytes 131104 | tf_op jit(solution)/shard_map/ppermute | solution.py:411
  38.4 0.1 added.7
  38.5 1.5 %far_part.2.own.after = bf16[1024,512]{1,0:T(8,128)(2,1)S(1)} custom-call(s32[1]{0:T(128)} %bitcast.device, bf16[4,128,128]{2,1,0:T(8,128)(2,1)S(1)} %get-tuple-element.123.after.refs_10_, f32[1,512]{1,0:T(1,128)S(1)} %bitcast.9, f32[512,512]{1,0:T(8,128)S(1)} %get-tuple-element.124.refs_0_, bf16[512,512]{1,0:T(8,128)(2,1)S(1)} %get-tuple-element.125.refs_1_, ...), custom_call_target="tpu_custom_call" | custom-call | flops 536870912 | bytes 5242880 | tf_op jit(solution)/shard_map/far_part/pallas_call | solution.py:283
  40.0 0.1 collective-permute-start.7
  40.0 1.3 %collective-permute-start.9 = (bf16[4,128,128]{2,1,0:T(8,128)(2,1)S(1)}, bf16[4,128,128]{2,1,0:T(8,128)(2,1)S(1)}, u32[]{:S(2)}, u32[]{:S(2)}) collective-permute-start(bf16[4,128,128]{2,1,0:T(8,128)(2,1)S(1)} %get-tuple-element.137), channel_id=1, source_target_pairs={{0,96},{8,104},{16,112},{24,120},{32,64},{40,72},{48,80},{56,88},{... | collective-permute-start | bytes 393224 | tf_op jit(solution)/shard_map/ppermute | solution.py:411
  41.3 2.9 %near_part.7 = (f32[512,512]{1,0:T(8,128)S(1)}, bf16[512,512]{1,0:T(8,128)(2,1)S(1)}, f32[68,512]{1,0:T(8,128)S(1)}) custom-call(bf16[2048,2048]{1,0:T(8,128)(2,1)S(1)} %get-tuple-element.114.tok, bf16[2048,512]{1,0:T(8,128)(2,1)S(1)} %get-tuple-element.93.wq, bf16[1024,512]{1,0:T(8,128)(2,1)S(1)} %get-tuple-element.115.keys, ...), custom_call_target="tpu_custom_call" | custom-call | flops 2147483648 | bytes 14680064 | tf_op jit(solution)/shard_map/near_part/pallas_call | solution.py:230
  44.2 2.3 %project.2 = (bf16[512,256]{1,0:T(8,128)(2,1)S(1)}, bf16[512,256]{1,0:T(8,128)(2,1)S(1)}, bf16[512,256]{1,0:T(8,128)(2,1)S(1)}, bf16[512,256]{1,0:T(8,128)(2,1)S...) custom-call(s32[1]{0:T(128)} %bitcast.1.group, ...), custom_call_target="tpu_custom_call" | custom-call | flops 2147483648 | bytes 4194304 | tf_op jit(solution)/shard_map/project/pallas_call | solution.py:312
  46.6 0.6 collective-permute-done.9.refs_9_
  47.2 1.7 %far_part.3.own = bf16[1024,512]{1,0:T(8,128)(2,1)S(1)} custom-call(s32[1]{0:T(128)} %bitcast.device, bf16[512,256]{1,0:T(8,128)(2,1)S(1)} %get-tuple-element.130.after, f32[1,512]{1,0:T(1,128)S(1)} %bitcast.10, f32[512,512]{1,0:T(8,128)S(1)} %get-tuple-element.131.refs_0_, bf16[512,512]{1,0:T(8,128)(2,1)S(1)} %get-tuple-element.132.refs_1_, ...), custom_call_target="tpu_custom_call" | custom-call | flops 671088640 | bytes 5242880 | tf_op jit(solution)/shard_map/far_part/pallas_call | solution.py:283
  48.9 0.1 collective-permute-start.10
  49.0 1.9 %collective-permute-start.14 = (bf16[512,256]{1,0:T(8,128)(2,1)S(1)}, bf16[512,256]{1,0:T(8,128)(2,1)S(1)}, u32[]{:S(2)}, u32[]{:S(2)}) collective-permute-start(bf16[512,256]{1,0:T(8,128)(2,1)S(1)} %get-tuple-element.130.after), channel_id=1, source_target_pairs={{0,2},{1,3},{2,4},{3,5},{4,6},{5,7},{6,0},{7,1},{8,10},{9,11},{10,... | collective-permute-start | bytes 786440 | tf_op jit(solution)/shard_map/ppermute | solution.py:398
  50.9 1.7 %collective-permute-start.15 = (bf16[512,256]{1,0:T(8,128)(2,1)S(1)}, bf16[512,256]{1,0:T(8,128)(2,1)S(1)}, u32[]{:S(2)}, u32[]{:S(2)}) collective-permute-start(bf16[512,256]{1,0:T(8,128)(2,1)S(1)} %get-tuple-element.146), channel_id=1, source_target_pairs={{0,6},{1,7},{2,0},{3,1},{4,2},{5,3},{6,4},{7,5},{8,14},{9,15},{10,... | collective-permute-start | bytes 786440 | tf_op jit(solution)/shard_map/ppermute | solution.py:398
  52.5 2.4 %project.3 = (bf16[512,256]{1,0:T(8,128)(2,1)S(1)}, bf16[512,256]{1,0:T(8,128)(2,1)S(1)}, bf16[512,256]{1,0:T(8,128)(2,1)S(1)}, bf16[512,256]{1,0:T(8,128)(2,1)S...) custom-call(s32[1]{0:T(128)} %bitcast.1.group, ...), custom_call_target="tpu_custom_call" | custom-call | flops 2147483648 | bytes 4194304 | tf_op jit(solution)/shard_map/project/pallas_call | solution.py:312
  54.9 0.8 collective-permute-start.11
  55.7 2.5 %collective-permute-start.12 = (bf16[512,256]{1,0:T(8,128)(2,1)S(1)}, bf16[512,256]{1,0:T(8,128)(2,1)S(1)}, u32[]{:S(2)}, u32[]{:S(2)}) collective-permute-start(bf16[512,256]{1,0:T(8,128)(2,1)S(1)} %get-tuple-element.142), channel_id=1, source_target_pairs={{0,6},{1,7},{2,0},{3,1},{4,2},{5,3},{6,4},{7,5},{8,14},{9,15},{10,... | collective-permute-start | bytes 786440 | tf_op jit(solution)/shard_map/ppermute | solution.py:398
  58.2 1.3 %collective-permute-done.14.from_down = bf16[512,256]{1,0:T(8,128)(2,1)S(1)} collective-permute-done((bf16[512,256]{1,0:T(8,128)(2,1)S(1)}, bf16[512,256]{1,0:T(8,128)(2,1)S(1)}, u32[]{:S(2)}, u32[]{:S(2)}) %collective-permute-start.14) | collective-permute-done | bytes 262176 | tf_op jit(solution)/shard_map/ppermute | solution.py:398
  59.5 0.4 collective-permute-done.15.from_up
  59.9 0.1 relay.3
  60.1 2.6 %collective-permute-start.16 = (bf16[1024,256]{1,0:T(8,128)(2,1)S(1)}, bf16[1024,256]{1,0:T(8,128)(2,1)S(1)}, u32[]{:S(2)}, u32[]{:S(2)}) collective-permute-start(bf16[1024,256]{1,0:T(8,128)(2,1)S(1)} %get-tuple-element.149), channel_id=1, source_target_pairs={{0,6},{1,7},{2,0},{3,1},{4,2},{5,3},{6,4},{7,5},{8,14},{9,15},{10,... | collective-permute-start | bytes 1572872 | tf_op jit(solution)/shard_map/ppermute | solution.py:398
  62.7 3.2 %collective-permute-start.19 = (bf16[512,256]{1,0:T(8,128)(2,1)S(1)}, bf16[512,256]{1,0:T(8,128)(2,1)S(1)}, u32[]{:S(2)}, u32[]{:S(2)}) collective-permute-start(bf16[512,256]{1,0:T(8,128)(2,1)S(1)} %get-tuple-element.154), channel_id=1, source_target_pairs={{0,6},{1,7},{2,0},{3,1},{4,2},{5,3},{6,4},{7,5},{8,14},{9,15},{10,... | collective-permute-start | bytes 786440 | tf_op jit(solution)/shard_map/ppermute | solution.py:398
  65.9 0.1 relay.2
  66.0 1.4 %collective-permute-start.13 = (bf16[512,256]{1,0:T(8,128)(2,1)S(1)}, bf16[512,256]{1,0:T(8,128)(2,1)S(1)}, u32[]{:S(2)}, u32[]{:S(2)}) collective-permute-start(bf16[512,256]{1,0:T(8,128)(2,1)S(1)} %get-tuple-element.143), channel_id=1, source_target_pairs={{0,2},{1,3},{2,4},{3,5},{4,6},{5,7},{6,0},{7,1},{8,10},{9,11},{10,... | collective-permute-start | bytes 786440 | tf_op jit(solution)/shard_map/ppermute | solution.py:398
  67.4 14.0 %collective-permute-done.19.refs_2_ = bf16[512,256]{1,0:T(8,128)(2,1)S(1)} collective-permute-done((bf16[512,256]{1,0:T(8,128)(2,1)S(1)}, bf16[512,256]{1,0:T(8,128)(2,1)S(1)}, u32[]{:S(2)}, u32[]{:S(2)}) %collective-permute-start.19) | collective-permute-done | bytes 262176 | tf_op jit(solution)/shard_map/ppermute | solution.py:398
  81.5 2.9 %collective-permute-start.18 = (bf16[512,256]{1,0:T(8,128)(2,1)S(1)}, bf16[512,256]{1,0:T(8,128)(2,1)S(1)}, u32[]{:S(2)}, u32[]{:S(2)}) collective-permute-start(bf16[512,256]{1,0:T(8,128)(2,1)S(1)} %get-tuple-element.152), channel_id=1, source_target_pairs={{0,6},{1,7},{2,0},{3,1},{4,2},{5,3},{6,4},{7,5},{8,14},{9,15},{10,... | collective-permute-start | bytes 786440 | tf_op jit(solution)/shard_map/ppermute | solution.py:398
  84.4 0.9 final.2.refs_6_
  85.3 1.9 %collective-permute-done.13.refs_1_ = bf16[512,256]{1,0:T(8,128)(2,1)S(1)} collective-permute-done((bf16[512,256]{1,0:T(8,128)(2,1)S(1)}, bf16[512,256]{1,0:T(8,128)(2,1)S(1)}, u32[]{:S(2)}, u32[]{:S(2)}) %collective-permute-start.13) | collective-permute-done | bytes 262176 | tf_op jit(solution)/shard_map/ppermute | solution.py:398
  87.3 1.9 %collective-permute-done.18.refs_5_ = bf16[512,256]{1,0:T(8,128)(2,1)S(1)} collective-permute-done((bf16[512,256]{1,0:T(8,128)(2,1)S(1)}, bf16[512,256]{1,0:T(8,128)(2,1)S(1)}, u32[]{:S(2)}, u32[]{:S(2)}) %collective-permute-start.18) | collective-permute-done | bytes 262176 | tf_op jit(solution)/shard_map/ppermute | solution.py:398
  89.2 0.9 final.3
  (18 shorter events, 0.1 us)
Async XLA Ops:
  0.0 9.6 %copy-start.2 = (bf16[512,2048]{1,0:T(8,128)(2,1)S(1)}, bf16[512,2048]{1,0:T(8,128)(2,1)}, u32[]{:S(2)}) copy-start(bf16[512,2048]{1,0:T(8,128)(2,1)} %w_own.3) | copy-start | bytes 6291460
  7.9 6.7 %collective-permute-start = (bf16[4,128,128]{2,1,0:T(8,128)(2,1)S(1)}, bf16[4,128,128]{2,1,0:T(8,128)(2,1)S(1)}, u32[]{:S(2)}, u32[]{:S(2)}) collective-permute-start(bf16[4,128,128]{2,1,0:T(8,128)(2,1)S(1)} %get-tuple-element.85.refs_0_), channel_id=1, source_target_pairs={{0,8},{8,0},{16,24},{24,16},{32,40},{40,32},{48,56},{56,48},{64,72... | collective-permute-start | bytes 393224 | tf_op jit(solution)/shard_map/ppermute | solution.py:411
  9.6 34.6 %collective-permute-start.8 = (bf16[512,2048]{1,0:T(8,128)(2,1)S(1)}, bf16[512,2048]{1,0:T(8,128)(2,1)S(1)}, u32[]{:S(2)}, u32[]{:S(2)}) collective-permute-start(bf16[512,2048]{1,0:T(8,128)(2,1)S(1)} %copy-done.2), channel_id=1, source_target_pairs={{0,1},{1,0},{2,3},{3,2},{4,5},{5,4},{6,7},{7,6},{8,9},{9,8},{10,11... | collective-permute-start | bytes 6291464 | tf_op jit(solution)/shard_map/ppermute | solution.py:395
  9.6 7.9 %copy-start = (bf16[4,128,17]{1,0,2:T(4,128)(2,1)S(1)}, bf16[4,128,17]{1,0,2:T(4,128)(2,1)}, u32[]{:S(2)}) copy-start(bf16[4,128,17]{1,0,2:T(4,128)(2,1)} %param.7) | copy-start | bytes 52228
  14.7 7.2 %collective-permute-start.1 = (bf16[4,128,128]{2,1,0:T(8,128)(2,1)S(1)}, bf16[4,128,128]{2,1,0:T(8,128)(2,1)S(1)}, u32[]{:S(2)}, u32[]{:S(2)}) collective-permute-start(bf16[4,128,128]{2,1,0:T(8,128)(2,1)S(1)} %added.4.after.refs_0_), channel_id=1, source_target_pairs={{0,24},{8,16},{16,8},{24,0},{32,56},{40,48},{48,40},{56,32},{64,88... | collective-permute-start | bytes 393224 | tf_op jit(solution)/shard_map/ppermute | solution.py:411
  16.9 5.6 %collective-permute-start.2 = (bf16[4,128,128]{2,1,0:T(8,128)(2,1)S(1)}, bf16[4,128,128]{2,1,0:T(8,128)(2,1)S(1)}, u32[]{:S(2)}, u32[]{:S(2)}) collective-permute-start(bf16[4,128,128]{2,1,0:T(8,128)(2,1)S(1)} %get-tuple-element.91.refs_2_), channel_id=1, source_target_pairs={{0,8},{8,0},{16,24},{24,16},{32,40},{40,32},{48,56},{56,48},{64,72... | collective-permute-start | bytes 393224 | tf_op jit(solution)/shard_map/ppermute | solution.py:411
  22.6 6.4 %collective-permute-start.3 = (bf16[4,128,128]{2,1,0:T(8,128)(2,1)S(1)}, bf16[4,128,128]{2,1,0:T(8,128)(2,1)S(1)}, u32[]{:S(2)}, u32[]{:S(2)}) collective-permute-start(bf16[4,128,128]{2,1,0:T(8,128)(2,1)S(1)} %get-tuple-element.103.after.refs_0_), channel_id=1, source_target_pairs={{0,32},{8,40},{16,48},{24,56},{32,0},{40,8},{48,16},{56,24},{64,96... | collective-permute-start | bytes 393224 | tf_op jit(solution)/shard_map/ppermute | solution.py:411
  24.6 6.2 %collective-permute-start.4 = (bf16[4,128,128]{2,1,0:T(8,128)(2,1)S(1)}, bf16[4,128,128]{2,1,0:T(8,128)(2,1)S(1)}, u32[]{:S(2)}, u32[]{:S(2)}) collective-permute-start(bf16[4,128,128]{2,1,0:T(8,128)(2,1)S(1)} %get-tuple-element.104.refs_2_), channel_id=1, source_target_pairs={{0,24},{8,16},{16,8},{24,0},{32,56},{40,48},{48,40},{56,32},{64,88... | collective-permute-start | bytes 393224 | tf_op jit(solution)/shard_map/ppermute | solution.py:411
  30.8 6.4 %collective-permute-start.5 = (bf16[4,128,128]{2,1,0:T(8,128)(2,1)S(1)}, bf16[4,128,128]{2,1,0:T(8,128)(2,1)S(1)}, u32[]{:S(2)}, u32[]{:S(2)}) collective-permute-start(bf16[4,128,128]{2,1,0:T(8,128)(2,1)S(1)} %get-tuple-element.112.after.refs_0_), channel_id=1, source_target_pairs={{0,96},{8,104},{16,112},{24,120},{32,64},{40,72},{48,80},{56,88},{... | collective-permute-start | bytes 393224 | tf_op jit(solution)/shard_map/ppermute | solution.py:411
  33.4 5.0 %collective-permute-start.6 = (bf16[4,128,128]{2,1,0:T(8,128)(2,1)S(1)}, bf16[4,128,128]{2,1,0:T(8,128)(2,1)S(1)}, u32[]{:S(2)}, u32[]{:S(2)}) collective-permute-start(bf16[4,128,128]{2,1,0:T(8,128)(2,1)S(1)} %get-tuple-element.113.refs_2_), channel_id=1, source_target_pairs={{0,32},{8,40},{16,48},{24,56},{32,0},{40,8},{48,16},{56,24},{64,96... | collective-permute-start | bytes 393224 | tf_op jit(solution)/shard_map/ppermute | solution.py:411
  34.4 4.0 %copy-start.1 = (f32[512]{0:T(512)S(1)}, f32[512]{0:T(512)}, u32[]{:S(2)}) copy-start(f32[512]{0:T(512)} %param.8) | copy-start | bytes 6148
  40.0 4.3 %collective-permute-start.7 = (bf16[1024,512]{1,0:T(8,128)(2,1)S(1)}, bf16[1024,512]{1,0:T(8,128)(2,1)S(1)}, u32[]{:S(2)}, u32[]{:S(2)}) collective-permute-start(bf16[1024,512]{1,0:T(8,128)(2,1)S(1)} %far_part.2.own.after), channel_id=1, source_target_pairs={{0,1},{1,0},{2,3},{3,2},{4,5},{5,4},{6,7},{7,6},{8,9},{9,8},{10,11... | collective-permute-start | bytes 3145736 | tf_op jit(solution)/shard_map/ppermute | solution.py:395
  40.0 7.1 %collective-permute-start.9 = (bf16[4,128,128]{2,1,0:T(8,128)(2,1)S(1)}, bf16[4,128,128]{2,1,0:T(8,128)(2,1)S(1)}, u32[]{:S(2)}, u32[]{:S(2)}) collective-permute-start(bf16[4,128,128]{2,1,0:T(8,128)(2,1)S(1)} %get-tuple-element.137), channel_id=1, source_target_pairs={{0,96},{8,104},{16,112},{24,120},{32,64},{40,72},{48,80},{56,88},{... | collective-permute-start | bytes 393224 | tf_op jit(solution)/shard_map/ppermute | solution.py:411
  48.9 3.6 %collective-permute-start.10 = (bf16[1024,512]{1,0:T(8,128)(2,1)S(1)}, bf16[1024,512]{1,0:T(8,128)(2,1)S(1)}, u32[]{:S(2)}, u32[]{:S(2)}) collective-permute-start(bf16[1024,512]{1,0:T(8,128)(2,1)S(1)} %far_part.3.own), channel_id=1, source_target_pairs={{0,1},{1,0},{2,3},{3,2},{4,5},{5,4},{6,7},{7,6},{8,9},{9,8},{10,11... | collective-permute-start | bytes 3145736 | tf_op jit(solution)/shard_map/ppermute | solution.py:395
  49.0 10.5 %collective-permute-start.14 = (bf16[512,256]{1,0:T(8,128)(2,1)S(1)}, bf16[512,256]{1,0:T(8,128)(2,1)S(1)}, u32[]{:S(2)}, u32[]{:S(2)}) collective-permute-start(bf16[512,256]{1,0:T(8,128)(2,1)S(1)} %get-tuple-element.130.after), channel_id=1, source_target_pairs={{0,2},{1,3},{2,4},{3,5},{4,6},{5,7},{6,0},{7,1},{8,10},{9,11},{10,... | collective-permute-start | bytes 786440 | tf_op jit(solution)/shard_map/ppermute | solution.py:398
  50.9 9.1 %collective-permute-start.15 = (bf16[512,256]{1,0:T(8,128)(2,1)S(1)}, bf16[512,256]{1,0:T(8,128)(2,1)S(1)}, u32[]{:S(2)}, u32[]{:S(2)}) collective-permute-start(bf16[512,256]{1,0:T(8,128)(2,1)S(1)} %get-tuple-element.146), channel_id=1, source_target_pairs={{0,6},{1,7},{2,0},{3,1},{4,2},{5,3},{6,4},{7,5},{8,14},{9,15},{10,... | collective-permute-start | bytes 786440 | tf_op jit(solution)/shard_map/ppermute | solution.py:398
  54.9 11.0 %collective-permute-start.11 = (bf16[512,256]{1,0:T(8,128)(2,1)S(1)}, bf16[512,256]{1,0:T(8,128)(2,1)S(1)}, u32[]{:S(2)}, u32[]{:S(2)}) collective-permute-start(bf16[512,256]{1,0:T(8,128)(2,1)S(1)} %get-tuple-element.141), channel_id=1, source_target_pairs={{0,2},{1,3},{2,4},{3,5},{4,6},{5,7},{6,0},{7,1},{8,10},{9,11},{10,... | collective-permute-start | bytes 786440 | tf_op jit(solution)/shard_map/ppermute | solution.py:398
  55.7 10.3 %collective-permute-start.12 = (bf16[512,256]{1,0:T(8,128)(2,1)S(1)}, bf16[512,256]{1,0:T(8,128)(2,1)S(1)}, u32[]{:S(2)}, u32[]{:S(2)}) collective-permute-start(bf16[512,256]{1,0:T(8,128)(2,1)S(1)} %get-tuple-element.142), channel_id=1, source_target_pairs={{0,6},{1,7},{2,0},{3,1},{4,2},{5,3},{6,4},{7,5},{8,14},{9,15},{10,... | collective-permute-start | bytes 786440 | tf_op jit(solution)/shard_map/ppermute | solution.py:398
  60.1 24.3 %collective-permute-start.16 = (bf16[1024,256]{1,0:T(8,128)(2,1)S(1)}, bf16[1024,256]{1,0:T(8,128)(2,1)S(1)}, u32[]{:S(2)}, u32[]{:S(2)}) collective-permute-start(bf16[1024,256]{1,0:T(8,128)(2,1)S(1)} %get-tuple-element.149), channel_id=1, source_target_pairs={{0,6},{1,7},{2,0},{3,1},{4,2},{5,3},{6,4},{7,5},{8,14},{9,15},{10,... | collective-permute-start | bytes 1572872 | tf_op jit(solution)/shard_map/ppermute | solution.py:398
  62.7 21.8 %collective-permute-start.17 = (bf16[1024,256]{1,0:T(8,128)(2,1)S(1)}, bf16[1024,256]{1,0:T(8,128)(2,1)S(1)}, u32[]{:S(2)}, u32[]{:S(2)}) collective-permute-start(bf16[1024,256]{1,0:T(8,128)(2,1)S(1)} %get-tuple-element.151), channel_id=1, source_target_pairs={{0,2},{1,3},{2,4},{3,5},{4,6},{5,7},{6,0},{7,1},{8,10},{9,11},{10,... | collective-permute-start | bytes 1572872 | tf_op jit(solution)/shard_map/ppermute | solution.py:398
  62.7 18.8 %collective-permute-start.19 = (bf16[512,256]{1,0:T(8,128)(2,1)S(1)}, bf16[512,256]{1,0:T(8,128)(2,1)S(1)}, u32[]{:S(2)}, u32[]{:S(2)}) collective-permute-start(bf16[512,256]{1,0:T(8,128)(2,1)S(1)} %get-tuple-element.154), channel_id=1, source_target_pairs={{0,6},{1,7},{2,0},{3,1},{4,2},{5,3},{6,4},{7,5},{8,14},{9,15},{10,... | collective-permute-start | bytes 786440 | tf_op jit(solution)/shard_map/ppermute | solution.py:398
  65.9 18.5 %collective-permute-start.20 = (bf16[512,256]{1,0:T(8,128)(2,1)S(1)}, bf16[512,256]{1,0:T(8,128)(2,1)S(1)}, u32[]{:S(2)}, u32[]{:S(2)}) collective-permute-start(bf16[512,256]{1,0:T(8,128)(2,1)S(1)} %get-tuple-element.156), channel_id=1, source_target_pairs={{0,2},{1,3},{2,4},{3,5},{4,6},{5,7},{6,0},{7,1},{8,10},{9,11},{10,... | collective-permute-start | bytes 786440 | tf_op jit(solution)/shard_map/ppermute | solution.py:398
  66.0 21.2 %collective-permute-start.13 = (bf16[512,256]{1,0:T(8,128)(2,1)S(1)}, bf16[512,256]{1,0:T(8,128)(2,1)S(1)}, u32[]{:S(2)}, u32[]{:S(2)}) collective-permute-start(bf16[512,256]{1,0:T(8,128)(2,1)S(1)} %get-tuple-element.143), channel_id=1, source_target_pairs={{0,2},{1,3},{2,4},{3,5},{4,6},{5,7},{6,0},{7,1},{8,10},{9,11},{10,... | collective-permute-start | bytes 786440 | tf_op jit(solution)/shard_map/ppermute | solution.py:398
  81.5 7.7 %collective-permute-start.18 = (bf16[512,256]{1,0:T(8,128)(2,1)S(1)}, bf16[512,256]{1,0:T(8,128)(2,1)S(1)}, u32[]{:S(2)}, u32[]{:S(2)}) collective-permute-start(bf16[512,256]{1,0:T(8,128)(2,1)S(1)} %get-tuple-element.152), channel_id=1, source_target_pairs={{0,6},{1,7},{2,0},{3,1},{4,2},{5,3},{6,4},{7,5},{8,14},{9,15},{10,... | collective-permute-start | bytes 786440 | tf_op jit(solution)/shard_map/ppermute | solution.py:398

commit v2 on v1

--- a/solution.py
+++ b/solution.py
@@ -180,47 +180,63 @@
     near8 = bits_of(jnp.bitwise_xor(lane8, key8))
     causal8 = lane8 >= key8
     tile_group = jnp.bitwise_and(lax.broadcasted_iota(jnp.int32, (8, CHUNK), 1), TILE - 1) // 8
-    for head in range(heads):
-        cols = slice(head * dim, (head + 1) * dim)
+
+    def weights_of(head):
         rough = jnp.zeros((16, BLOCK), F32)
         for level in range(1, 5):
             rough = jnp.where(apart == level, row(head, level + 3, 16), rough)
-        steps_ref[...] = jnp.where(before, rough, 0.0)
+        steps_ref[head] = jnp.where(before, rough, 0.0)
         fine = row(head, 0, 8)
         for level in range(1, 4):
             fine = jnp.where(near8 == level, row(head, level, 8), fine)
-        fine = jnp.where(causal8, fine, 0.0)
-        pair = (states[0, head].astype(F32) + states[1, head].astype(F32)).astype(BF16)
-        for chunk in range(2):
-            at = slice(chunk * CHUNK, (chunk + 1) * CHUNK)
-            query = queries[at, cols]
-            left = [k_ref[at, cols]]
-            if step == 1:
-                left.append(pair)
-            if chunk == 1:
-                left.append(states[2 * step, head])
-            score = dot_nt(jnp.concatenate(left, axis=0), query)
-            top, bottom = [], []
-            across = row(head, 8, 8, slice(chunk * CHUNK + TILE, (chunk + 1) * CHUNK))
-            for j in range(16):
-                weight = jnp.where(
-                    tile_group == j, fine[:, at], steps_ref[pl.ds(j, 8, stride=0), :][:, at]
-                )
-                low = score[8 * j : 8 * j + 8]
-                high = score[TILE + 8 * j : TILE + 8 * j + 8, TILE:]
-                top.append(
-                    jnp.concatenate([low[:, :TILE] * weight[:, :TILE], low[:, TILE:] * across], axis=1)
-                )
-                bottom.append(
-                    jnp.concatenate([jnp.zeros((8, TILE), F32), high * weight[:, TILE:]], axis=1)
-                )
-            mixed = jnp.concatenate(top + bottom, axis=0).astype(BF16)
-            near = dot(vt_ref[cols, at], mixed)
-            wider = ([10] if step == 1 else []) + ([9] if chunk == 1 else [])
-            for order, level in enumerate(wider):
-                scale = jnp.concatenate([row(head, level, 8, at)] * (dim // 8), axis=0)
-                near = near + scale * score[CHUNK + order * dim : CHUNK + (order + 1) * dim]
-            near_out[cols, at] = near
+        return jnp.where(causal8, fine, 0.0)
+
+    def scores_of(head, chunk):
+        cols = slice(head * dim, (head + 1) * dim)
+        at = slice(chunk * CHUNK, (chunk + 1) * CHUNK)
+        left = [k_ref[at, cols]]
+        if step == 1:
+            left.append((states[0, head].astype(F32) + states[1, head].astype(F32)).astype(BF16))
+        if chunk == 1:
+            left.append(states[2 * step, head])
+        return dot_nt(jnp.concatenate(left, axis=0), queries[at, cols])
+
+    def mixed_of(head, chunk, score, fine):
+        at = slice(chunk * CHUNK, (chunk + 1) * CHUNK)
+        top, bottom = [], []
+        across = row(head, 8, 8, slice(chunk * CHUNK + TILE, (chunk + 1) * CHUNK))
+        for j in range(16):
+            weight = jnp.where(
+                tile_group == j, fine[:, at], steps_ref.at[head][pl.ds(j, 8, stride=0), :][:, at]
+            )
+            low = score[8 * j : 8 * j + 8]
+            high = score[TILE + 8 * j : TILE + 8 * j + 8, TILE:]
+            top.append(
+                jnp.concatenate([low[:, :TILE] * weight[:, :TILE], low[:, TILE:] * across], axis=1)
+            )
+            bottom.append(
+                jnp.concatenate([jnp.zeros((8, TILE), F32), high * weight[:, TILE:]], axis=1)
+            )
+        return jnp.concatenate(top + bottom, axis=0).astype(BF16)
+
+    def finish(head, chunk, score, mixed):
+        cols = slice(head * dim, (head + 1) * dim)
+        at = slice(chunk * CHUNK, (chunk + 1) * CHUNK)
+        near = dot(vt_ref[cols, at], mixed)
+        wider = ([10] if step == 1 else []) + ([9] if chunk == 1 else [])
+        for order, level in enumerate(wider):
+            scale = jnp.concatenate([row(head, level, 8, at)] * (dim // 8), axis=0)
+            near = near + scale * score[CHUNK + order * dim : CHUNK + (order + 1) * dim]
+        near_out[cols, at] = near
+
+    for first_head in range(0, heads, 2):
+        pair = (first_head, first_head + 1)
+        fines = {head: weights_of(head) for head in pair}
+        units = [(head, chunk) for head in pair for chunk in range(2)]
+        scores = [scores_of(*unit) for unit in units]
+        mixes = [mixed_of(*unit, score, fines[unit[0]]) for unit, score in zip(units, scores)]
+        for unit, score, mixed in zip(units, scores, mixes):
+            finish(*unit, score, mixed)
 
 
 def near_part(held, after, half, step, heads, dim):
@@ -236,7 +252,7 @@
             jax.ShapeDtypeStruct((BLOCK, width), BF16),
             jax.ShapeDtypeStruct((held[5].shape[0] * heads, BLOCK), F32),
         ],
-        scratch_shapes=[pltpu.VMEM((16, BLOCK), F32)],
+        scratch_shapes=[pltpu.VMEM((heads, 16, BLOCK), F32)],
         compiler_params=pltpu.CompilerParams(vmem_limit_bytes=SMALL << 20),
         cost_estimate=cost(4 * BLOCK * depth * width, 14),
         name="near_part",
@@ -293,9 +309,9 @@
     )(device, after, gain, *blocks, *states)
 
 
-def project_kernel(feats, ring, group, own, peer, w_own, w_peer, *outs):
+def project_kernel(feats, ring, shifts, group, own, peer, w_own, w_peer, *outs):
     block = own.shape[0] // 2
-    for order, shift in enumerate((2, 1, ring - 1, 0)):
+    for order, shift in enumerate(shifts):
         slot = 2 * (((group[0] >> 1) + shift) % ring) + (group[0] & 1)
         at = pl.ds(pl.multiple_of(slot * feats, feats), feats)
         for part in range(2):
@@ -305,17 +321,19 @@
             out[...] = total.astype(out.dtype)
 
 
-def project(group, ring, own, peer, w_own, w_peer, feats):
+def project(group, ring, own, peer, w_own, w_peer, feats, shifts):
     rows, width = own.shape
     vmem = pl.BlockSpec(memory_space=pltpu.VMEM)
     size = (rows // 2, feats)
     return pl.pallas_call(
-        functools.partial(project_kernel, feats, ring),
+        functools.partial(project_kernel, feats, ring, shifts),
         in_specs=[pl.BlockSpec(memory_space=pltpu.SMEM)] + [vmem] * 4,
-        out_specs=[vmem] * 8,
-        out_shape=[jax.ShapeDtypeStruct(size, BF16)] * 6 + [jax.ShapeDtypeStruct(size, F32)] * 2,
+        out_specs=[vmem] * (2 * len(shifts)),
+        out_shape=[
+            jax.ShapeDtypeStruct(size, BF16 if shift else F32) for shift in shifts for _ in range(2)
+        ],
         compiler_params=pltpu.CompilerParams(vmem_limit_bytes=12 << 20),
-        cost_estimate=cost(16 * rows * width * feats, 4),
+        cost_estimate=cost(4 * rows * width * feats * len(shifts), 4),
         name="project",
     )(group, own, peer, w_own, w_peer)
 
@@ -422,64 +440,58 @@
     def step_of(half, mask):
         return over_ctx(sums[half], mask)
 
-    def advance(**arrived):
-        names = {"low": 0, "high": 1}
-        fresh = added(*[(sums[names[name]], value) for name, value in arrived.items()])
-        for (name, value), total in zip(arrived.items(), fresh):
-            levels_of[names[name]].append(value)
-            sums[names[name]] = total
+    def advance(half, arrived):
+        levels_of[half].append(arrived)
+        sums[half] = added((sums[half], arrived))[0]
 
     near = {}
     masks = (1, 3, 4, 12)
-    low_x1 = step_of(0, masks[0])
+    low = step_of(0, masks[0])
     high = key_value(heads, dim, half_rows, (rows, weight_k, weight_v), False)
     held[1] = (rows, weight_q, *high[:3], gate_w)
     sums[1] = high[3]
-    low_x1, sums[1] = lax.optimization_barrier((low_x1, sums[1]))
-    advance(low=low_x1)
-    low_x3, high_x1 = step_of(0, masks[1]), step_of(1, masks[0])
-
-    def block_after(half, step, value):
-        start, *others = held[half]
-        start, value = lax.optimization_barrier((start, value))
-        near[half, step] = near_part((start, *others), value, half, step, heads, dim)
-        return value
-
-    sums[0] = block_after(0, 0, sums[0])
-    low_x3, high_x1, near[0, 0] = lax.optimization_barrier((low_x3, high_x1, near[0, 0]))
-    advance(low=low_x3, high=high_x1)
-    low_z1, high_x3 = step_of(0, masks[2]), step_of(1, masks[1])
-    sums[0] = block_after(0, 1, sums[0])
-    low_z1, high_x3, near[0, 1] = lax.optimization_barrier((low_z1, high_x3, near[0, 1]))
-    advance(low=low_z1, high=high_x3)
-    low_z3, high_z1 = step_of(0, masks[3]), step_of(1, masks[2])
-    sums[0] = block_after(1, 0, sums[0])
-    low_z3, high_z1, near[1, 0] = lax.optimization_barrier((low_z3, high_z1, near[1, 0]))
-    advance(low=low_z3, high=high_z1)
-    high_z3 = step_of(1, masks[3])
-    levels_of[1].append(high_z3)
-    levels_of[1].append(sums[0])
+    low, sums[1] = lax.optimization_barrier((low, sums[1]))
+    high = step_of(1, masks[0])
+    advance(0, low)
+    low = step_of(0, masks[1])
+    for index, (half, step) in enumerate(((0, 0), (0, 1), (1, 0))):
+        after = sums[0] if index == 0 else sums[1]
+        make = lambda: near_part(held[half], after, half, step, heads, dim)
+        near[half, step] = make()
+        low, near[half, step] = lax.optimization_barrier((low, near[half, step]))
+        if index == 2:
+            break
+        advance(0, low)
+        low = step_of(0, masks[index + 2])
+        advance(1, high)
+        high = step_of(1, masks[index + 1])
+    levels_of[0].append(low)
 
     def attended(half, after):
         parts = [near[half, 0], near[half, 1]]
         return far_part(where_ctx, after, parts, gain, levels_of[half], heads, dim, level0)
 
-    def sent(own, peer):
-        return project(where_head, ring, own, peer, output_weight, peer_weight, feats)
+    def sent(own, peer, *shifts):
+        return project(where_head, ring, own, peer, output_weight, peer_weight, feats, shifts)
 
     def sent_over(value, shift):
         return over_ring(value, shift)
 
-    own_low = attended(0, sums[0])
+    own_low = attended(0, near[1, 0][2])
     peer_low = over_core(own_low)
+    advance(1, high)
+    levels_of[1].append(step_of(1, masks[3]))
+    levels_of[1].append(added((sums[0], low))[0])
     near[1, 1] = near_part(held[1], own_low, 1, 1, heads, dim)
-    top, bottom, up_a, up_b, down_a, down_b, low_a, low_b = sent(own_low, peer_low)
+    top, bottom = sent(own_low, peer_low, 2)
     low_pair = [sent_over(top, 1), sent_over(bottom, -1)]
     own_high = attended(1, top)
+    up_a, up_b, down_a, down_b, low_a, low_b = sent(own_low, peer_low, 1, ring - 1, 0)
     low_up_b, low_down_a = sent_over(up_b, 1), sent_over(down_a, -1)
     peer_high = over_core(own_high)
-    top, bottom, high_up_a, high_up_b, high_down_a, high_down_b, high_a, high_b = sent(own_high, peer_high)
+    top, bottom = sent(own_high, peer_high, 2)
     high_pair = [sent_over(top, 1), sent_over(bottom, -1)]
+    high_up_a, high_up_b, high_down_a, high_down_b, high_a, high_b = sent(own_high, peer_high, 1, ring - 1, 0)
     up_mix, down_mix = relay(up_a, down_b, *low_pair, high_up_b, high_down_a)
     up_mix, down_mix = sent_over(up_mix, 1), sent_over(down_mix, -1)
     up_last, down_last = relay(high_up_a, high_down_b, *high_pair)

time: 91 us -> 92.3 us (1.014)
  waiting for transfers between devices: 25.5 us -> 27.8 us
  Pallas kernels: 34.3 us -> 32.4 us
  starting transfers between devices: 30 us -> 31 us
    ppermute x8, waiting for transfers between devices: 5.88 us -> 9.78 us  [over_ctx(): return lax.ppermute(value, 'ctx', [(i, i ^ mask) for i in range(ctx_count)])]
    pallas_call x4, Pallas kernels: 11.2 us -> 8.88 us  [near_part(): pl.pallas_call(functools.partial(near_kernel, heads, dim, half, step), in...]
    ppermute x10, waiting for transfers between devices: 19.7 us -> 18 us  [over_ring(): lax.ppermute(value, 'head', [(i, (i + 2 * shift) % head_count) for i in r...]
    ppermute x8, starting transfers between devices: 12.9 us -> 14.4 us  [over_ctx(): return lax.ppermute(value, 'ctx', [(i, i ^ mask) for i in range(ctx_count)])]
    pallas_call x2 -> x4, Pallas kernels: 4.71 us -> 5.04 us  [project(): pl.pallas_call(functools.partial(project_kernel, feats, ring, shifts), in...]
  transfers between devices with their start and end apart: 21 -> 21, of which waited for: 10 -> 7; matrix products, arithmetic and copies ran while one was open for 0% -> 0% of each run, Pallas kernels for 26% -> 24%
where the time goes in v2:
time: 92.3 us; the launch traced here: 91.6 us
  Pallas kernels  32.4 us (35%)
  starting transfers between devices  31 us (34%)
  waiting for transfers between devices  27.8 us (30%)
    ppermute x10, waiting for transfers between devices, over_ring(): lax.ppermute(value, 'head', [(i, (i + 2 * shift) % head_count) for i in r...  18 us
    ppermute x10, starting transfers between devices, over_ring(): lax.ppermute(value, 'head', [(i, (i + 2 * shift) % head_count) for i in r...  16.5 us
    ppermute x8, starting transfers between devices, over_ctx(): return lax.ppermute(value, 'ctx', [(i, i ^ mask) for i in range(ctx_count)])  14.4 us
    pallas_call x2, Pallas kernels, key_value(): pl.pallas_call(functools.partial(first_kernel if first else second_kernel...  12.9 us
    ppermute x8, waiting for transfers between devices, over_ctx(): return lax.ppermute(value, 'ctx', [(i, i ^ mask) for i in range(ctx_count)])  9.78 us
    pallas_call x4, Pallas kernels, near_part(): pl.pallas_call(functools.partial(near_kernel, heads, dim, half, step), in...  8.88 us
    pallas_call x4, Pallas kernels, project(): pl.pallas_call(functools.partial(project_kernel, feats, ring, shifts), in...  5.04 us
    pallas_call x2, Pallas kernels, far_part(): pl.pallas_call(functools.partial(far_kernel, heads, dim, level0, count, c...  3.21 us
  transfers between devices with their start and end apart: 21, of which 7 were waited for; matrix products, arithmetic and copies ran while one was open for 0% of the time, Pallas kernels for 24%

profile of v2, /device:TPU:0, one launch (start us, length us, event | category | flops | bytes accessed | tf_op | source)
XLA Modules:
  0.0 91.6 jit_solution(7759994455956601820)
XLA Ops:
  0.0 7.9 %key_value.2 = (bf16[1024,512]{1,0:T(8,128)(2,1)S(1)}, bf16[2,512,512]{2,1,0:T(8,128)(2,1)S(1)}, bf16[4,4,128,128]{3,2,1,0:T(8,128)(2,1)S(1)}, bf16[4,128,128]{2...) custom-call(bf16[2048,2048]{1,0:T(8,128)(2,1)} %tok_in, ...), custom_call_target="tpu_custom_call" | custom-call | flops 4294967296 | bytes 14680064 | tf_op jit(solution)/shard_map/key_value/pallas_call | solution.py:118
  7.9 1.7 %collective-permute-start = (bf16[4,128,128]{2,1,0:T(8,128)(2,1)S(1)}, bf16[4,128,128]{2,1,0:T(8,128)(2,1)S(1)}, u32[]{:S(2)}, u32[]{:S(2)}) collective-permute-start(bf16[4,128,128]{2,1,0:T(8,128)(2,1)S(1)} %get-tuple-element.69.refs_0_), channel_id=1, source_target_pairs={{0,8},{8,0},{16,24},{24,16},{32,40},{40,32},{48,56},{56,48},{64,72... | collective-permute-start | bytes 393224 | tf_op jit(solution)/shard_map/ppermute | solution.py:429
  9.6 0.0 collective-permute-start.7
  9.6 5.0 %key_value.3 = (bf16[1024,512]{1,0:T(8,128)(2,1)S(1)}, bf16[2,512,512]{2,1,0:T(8,128)(2,1)S(1)}, bf16[4,4,128,128]{3,2,1,0:T(8,128)(2,1)S(1)}, bf16[4,128,128]{2,1,0:T(8,128)(2,1)S(1)}) custom-call(bf16[2048,2048]{1,0:T(8,128)(2,1)S(1)} %get-tuple-element.70.tok, bf16[2048,512]{1,0:T(8,128)(2,1)S(1)} %get-tuple-element.71.wk, ...), custom_call_target="tpu_custom_call" | custom-call | flops 4294967296 | bytes 14680064 | tf_op jit(solution)/shard_map/key_value/pallas_call | solution.py:118
  14.7 2.2 %collective-permute-start.1 = (bf16[4,128,128]{2,1,0:T(8,128)(2,1)S(1)}, bf16[4,128,128]{2,1,0:T(8,128)(2,1)S(1)}, u32[]{:S(2)}, u32[]{:S(2)}) collective-permute-start(bf16[4,128,128]{2,1,0:T(8,128)(2,1)S(1)} %added.7.after.refs_0_), channel_id=1, source_target_pairs={{0,24},{8,16},{16,8},{24,0},{32,56},{40,48},{48,40},{56,32},{64,88... | collective-permute-start | bytes 393224 | tf_op jit(solution)/shard_map/ppermute | solution.py:429
  16.9 0.6 collective-permute-start.3
  17.5 2.2 %near_part.4 = (f32[512,512]{1,0:T(8,128)S(1)}, bf16[512,512]{1,0:T(8,128)(2,1)S(1)}, f32[68,512]{1,0:T(8,128)S(1)}) custom-call(bf16[2048,2048]{1,0:T(8,128)(2,1)S(1)} %get-tuple-element.70.tok, bf16[2048,512]{1,0:T(8,128)(2,1)S(1)} %get-tuple-element.75.wq, bf16[1024,512]{1,0:T(8,128)(2,1)S(1)} %get-tuple-element.76.keys, ...), custom_call_target="tpu_custom_call" | custom-call | flops 2147483648 | bytes 14680064 | tf_op jit(solution)/shard_map/near_part/pallas_call | solution.py:246
  19.7 2.2 %collective-permute-done.1.refs_1_.refs_7_ = bf16[4,128,128]{2,1,0:T(8,128)(2,1)S(1)} collective-permute-done((bf16[4,128,128]{2,1,0:T(8,128)(2,1)S(1)}, bf16[4,128,128]{2,1,0:T(8,128)(2,1)S(1)}, u32[]{:S(2)}, u32[]{:S(2)}) %collective-permute-start.1) | collective-permute-done | bytes 131104 | tf_op jit(solution)/shard_map/ppermute | solution.py:429
  21.9 2.0 %collective-permute-start.2 = (bf16[4,128,128]{2,1,0:T(8,128)(2,1)S(1)}, bf16[4,128,128]{2,1,0:T(8,128)(2,1)S(1)}, u32[]{:S(2)}, u32[]{:S(2)}) collective-permute-start(bf16[4,128,128]{2,1,0:T(8,128)(2,1)S(1)} %added.8.refs_0_), channel_id=1, source_target_pairs={{0,32},{8,40},{16,48},{24,56},{32,0},{40,8},{48,16},{56,24},{64,96... | collective-permute-start | bytes 393224 | tf_op jit(solution)/shard_map/ppermute | solution.py:429
  23.9 0.0 collective-permute-done.3.refs_1_.refs_6_
  24.0 2.4 %collective-permute-start.5 = (bf16[4,128,128]{2,1,0:T(8,128)(2,1)S(1)}, bf16[4,128,128]{2,1,0:T(8,128)(2,1)S(1)}, u32[]{:S(2)}, u32[]{:S(2)}) collective-permute-start(bf16[4,128,128]{2,1,0:T(8,128)(2,1)S(1)} %added.9.after.refs_0_), channel_id=1, source_target_pairs={{0,24},{8,16},{16,8},{24,0},{32,56},{40,48},{48,40},{56,32},{64,88... | collective-permute-start | bytes 393224 | tf_op jit(solution)/shard_map/ppermute | solution.py:429
  26.3 2.3 %near_part.5 = (f32[512,512]{1,0:T(8,128)S(1)}, bf16[512,512]{1,0:T(8,128)(2,1)S(1)}, f32[68,512]{1,0:T(8,128)S(1)}) custom-call(bf16[2048,2048]{1,0:T(8,128)(2,1)S(1)} %get-tuple-element.70.tok, bf16[2048,512]{1,0:T(8,128)(2,1)S(1)} %get-tuple-element.75.wq, bf16[1024,512]{1,0:T(8,128)(2,1)S(1)} %get-tuple-element.76.keys, ...), custom_call_target="tpu_custom_call" | custom-call | flops 2147483648 | bytes 14680064 | tf_op jit(solution)/shard_map/near_part/pallas_call | solution.py:246
  28.6 2.6 %collective-permute-start.4 = (bf16[4,128,128]{2,1,0:T(8,128)(2,1)S(1)}, bf16[4,128,128]{2,1,0:T(8,128)(2,1)S(1)}, u32[]{:S(2)}, u32[]{:S(2)}) collective-permute-start(bf16[4,128,128]{2,1,0:T(8,128)(2,1)S(1)} %added.10.refs_0_), channel_id=1, source_target_pairs={{0,96},{8,104},{16,112},{24,120},{32,64},{40,72},{48,80},{56,88},{... | collective-permute-start | bytes 393224 | tf_op jit(solution)/shard_map/ppermute | solution.py:429
  31.3 0.0 copy-start.2
  31.3 2.2 %near_part.6 = (f32[512,512]{1,0:T(8,128)S(1)}, bf16[512,512]{1,0:T(8,128)(2,1)S(1)}, f32[68,512]{1,0:T(8,128)S(1)}) custom-call(bf16[2048,2048]{1,0:T(8,128)(2,1)S(1)} %get-tuple-element.70.tok, bf16[2048,512]{1,0:T(8,128)(2,1)S(1)} %get-tuple-element.75.wq, bf16[1024,512]{1,0:T(8,128)(2,1)S(1)} %get-tuple-element.88.keys, ...), custom_call_target="tpu_custom_call" | custom-call | flops 2147483648 | bytes 14680064 | tf_op jit(solution)/shard_map/near_part/pallas_call | solution.py:246
  33.5 1.4 %collective-permute-done.4.refs_9_.refs_1_ = bf16[4,128,128]{2,1,0:T(8,128)(2,1)S(1)} collective-permute-done((bf16[4,128,128]{2,1,0:T(8,128)(2,1)S(1)}, bf16[4,128,128]{2,1,0:T(8,128)(2,1)S(1)}, u32[]{:S(2)}, u32[]{:S(2)}) %collective-permute-start.4) | collective-permute-done | bytes 131104 | tf_op jit(solution)/shard_map/ppermute | solution.py:429
  34.9 1.5 %far_part.2.own.after = bf16[1024,512]{1,0:T(8,128)(2,1)S(1)} custom-call(s32[1]{0:T(128)} %bitcast.device, f32[68,512]{1,0:T(8,128)S(1)} %get-tuple-element.94.after.refs_2_, f32[1,512]{1,0:T(1,128)S(1)} %bitcast.9, f32[512,512]{1,0:T(8,128)S(1)} %get-tuple-element.95.refs_0_, bf16[512,512]{1,0:T(8,128)(2,1)S(1)} %get-tuple-element.96.refs_1_, ...), custom_call_target="tpu_custom_call" | custom-call | flops 536870912 | bytes 5242880 | tf_op jit(solution)/shard_map/far_part/pallas_call | solution.py:299
  36.4 0.1 collective-permute-start.6
  36.5 0.4 collective-permute-start.8
  36.9 5.5 %collective-permute-done.8.refs_1_.refs_8_ = bf16[4,128,128]{2,1,0:T(8,128)(2,1)S(1)} collective-permute-done((bf16[4,128,128]{2,1,0:T(8,128)(2,1)S(1)}, bf16[4,128,128]{2,1,0:T(8,128)(2,1)S(1)}, u32[]{:S(2)}, u32[]{:S(2)}) %collective-permute-start.8) | collective-permute-done | bytes 131104 | tf_op jit(solution)/shard_map/ppermute | solution.py:429
  42.4 2.6 %collective-permute-start.9 = (bf16[4,128,128]{2,1,0:T(8,128)(2,1)S(1)}, bf16[4,128,128]{2,1,0:T(8,128)(2,1)S(1)}, u32[]{:S(2)}, u32[]{:S(2)}) collective-permute-start(bf16[4,128,128]{2,1,0:T(8,128)(2,1)S(1)} %added.12), channel_id=1, source_target_pairs={{0,96},{8,104},{16,112},{24,120},{32,64},{40,72},{48,80},{56,88},{... | collective-permute-start | bytes 393224 | tf_op jit(solution)/shard_map/ppermute | solution.py:429
  45.0 2.3 %near_part.7 = (f32[512,512]{1,0:T(8,128)S(1)}, bf16[512,512]{1,0:T(8,128)(2,1)S(1)}, f32[68,512]{1,0:T(8,128)S(1)}) custom-call(bf16[2048,2048]{1,0:T(8,128)(2,1)S(1)} %get-tuple-element.70.tok, bf16[2048,512]{1,0:T(8,128)(2,1)S(1)} %get-tuple-element.75.wq, bf16[1024,512]{1,0:T(8,128)(2,1)S(1)} %get-tuple-element.88.keys, ...), custom_call_target="tpu_custom_call" | custom-call | flops 2147483648 | bytes 14680064 | tf_op jit(solution)/shard_map/near_part/pallas_call | solution.py:246
  47.3 0.0 collective-permute-done.6.peer
  47.3 0.7 project.4
  48.0 0.6 collective-permute-done.9.refs_9_
  48.7 1.7 %far_part.3.own = bf16[1024,512]{1,0:T(8,128)(2,1)S(1)} custom-call(s32[1]{0:T(128)} %bitcast.device, bf16[512,256]{1,0:T(8,128)(2,1)S(1)} %get-tuple-element.102.after, f32[1,512]{1,0:T(1,128)S(1)} %bitcast.10, f32[512,512]{1,0:T(8,128)S(1)} %get-tuple-element.103.refs_0_, bf16[512,512]{1,0:T(8,128)(2,1)S(1)} %get-tuple-element.104.refs_1_, ...), custom_call_target="tpu_custom_call" | custom-call | flops 671088640 | bytes 5242880 | tf_op jit(solution)/shard_map/far_part/pallas_call | solution.py:299
  50.4 0.1 collective-permute-start.10
  50.5 1.6 %collective-permute-start.14 = (bf16[512,256]{1,0:T(8,128)(2,1)S(1)}, bf16[512,256]{1,0:T(8,128)(2,1)S(1)}, u32[]{:S(2)}, u32[]{:S(2)}) collective-permute-start(bf16[512,256]{1,0:T(8,128)(2,1)S(1)} %get-tuple-element.102.after), channel_id=1, source_target_pairs={{0,2},{1,3},{2,4},{3,5},{4,6},{5,7},{6,0},{7,1},{8,10},{9,11},{10,... | collective-permute-start | bytes 786440 | tf_op jit(solution)/shard_map/ppermute | solution.py:416
  52.2 1.7 %collective-permute-start.15 = (bf16[512,256]{1,0:T(8,128)(2,1)S(1)}, bf16[512,256]{1,0:T(8,128)(2,1)S(1)}, u32[]{:S(2)}, u32[]{:S(2)}) collective-permute-start(bf16[512,256]{1,0:T(8,128)(2,1)S(1)} %get-tuple-element.116), channel_id=1, source_target_pairs={{0,6},{1,7},{2,0},{3,1},{4,2},{5,3},{6,4},{7,5},{8,14},{9,15},{10,... | collective-permute-start | bytes 786440 | tf_op jit(solution)/shard_map/ppermute | solution.py:416
  53.8 1.8 %project.7 = (bf16[512,256]{1,0:T(8,128)(2,1)S(1)}, bf16[512,256]{1,0:T(8,128)(2,1)S(1)}, bf16[512,256]{1,0:T(8,128)(2,1)S(1)}, bf16[512,256]{1,0:T(8,128)(2,1)S...) custom-call(s32[1]{0:T(128)} %bitcast.1.group, bf16[1024,512]{1,0:T(8,128)(2,1)S(1)} %far_part.2.own.after, ...), custom_call_target="tpu_custom_call" | custom-call | flops 1610612736 | bytes 4194304 | tf_op jit(solution)/shard_map/project/pallas_call | solution.py:328
  55.6 0.7 project.6
  56.3 0.7 collective-permute-start.11
  57.0 2.9 %collective-permute-start.12 = (bf16[512,256]{1,0:T(8,128)(2,1)S(1)}, bf16[512,256]{1,0:T(8,128)(2,1)S(1)}, u32[]{:S(2)}, u32[]{:S(2)}) collective-permute-start(bf16[512,256]{1,0:T(8,128)(2,1)S(1)} %get-tuple-element.112), channel_id=1, source_target_pairs={{0,6},{1,7},{2,0},{3,1},{4,2},{5,3},{6,4},{7,5},{8,14},{9,15},{10,... | collective-permute-start | bytes 786440 | tf_op jit(solution)/shard_map/ppermute | solution.py:416
  59.9 1.8 %project.5 = (bf16[512,256]{1,0:T(8,128)(2,1)S(1)}, bf16[512,256]{1,0:T(8,128)(2,1)S(1)}, bf16[512,256]{1,0:T(8,128)(2,1)S(1)}, bf16[512,256]{1,0:T(8,128)(2,1)S...) custom-call(s32[1]{0:T(128)} %bitcast.1.group, bf16[1024,512]{1,0:T(8,128)(2,1)S(1)} %far_part.3.own, ...), custom_call_target="tpu_custom_call" | custom-call | flops 1610612736 | bytes 4194304 | tf_op jit(solution)/shard_map/project/pallas_call | solution.py:328
  61.7 0.0 collective-permute-done.15.from_up
  61.7 0.1 relay.3
  61.9 1.9 %collective-permute-start.16 = (bf16[1024,256]{1,0:T(8,128)(2,1)S(1)}, bf16[1024,256]{1,0:T(8,128)(2,1)S(1)}, u32[]{:S(2)}, u32[]{:S(2)}) collective-permute-start(bf16[1024,256]{1,0:T(8,128)(2,1)S(1)} %get-tuple-element.119), channel_id=1, source_target_pairs={{0,6},{1,7},{2,0},{3,1},{4,2},{5,3},{6,4},{7,5},{8,14},{9,15},{10,... | collective-permute-start | bytes 1572872 | tf_op jit(solution)/shard_map/ppermute | solution.py:416
  63.7 0.2 collective-permute-start.17
  64.0 3.0 %collective-permute-start.19 = (bf16[512,256]{1,0:T(8,128)(2,1)S(1)}, bf16[512,256]{1,0:T(8,128)(2,1)S(1)}, u32[]{:S(2)}, u32[]{:S(2)}) collective-permute-start(bf16[512,256]{1,0:T(8,128)(2,1)S(1)} %get-tuple-element.124), channel_id=1, source_target_pairs={{0,6},{1,7},{2,0},{3,1},{4,2},{5,3},{6,4},{7,5},{8,14},{9,15},{10,... | collective-permute-start | bytes 786440 | tf_op jit(solution)/shard_map/ppermute | solution.py:416
  67.0 0.0 collective-permute-done.11.from_down
  67.0 0.1 relay.2
  67.1 1.6 %collective-permute-start.13 = (bf16[512,256]{1,0:T(8,128)(2,1)S(1)}, bf16[512,256]{1,0:T(8,128)(2,1)S(1)}, u32[]{:S(2)}, u32[]{:S(2)}) collective-permute-start(bf16[512,256]{1,0:T(8,128)(2,1)S(1)} %get-tuple-element.113), channel_id=1, source_target_pairs={{0,2},{1,3},{2,4},{3,5},{4,6},{5,7},{6,0},{7,1},{8,10},{9,11},{10,... | collective-permute-start | bytes 786440 | tf_op jit(solution)/shard_map/ppermute | solution.py:416
  68.7 14.3 %collective-permute-done.19.refs_2_ = bf16[512,256]{1,0:T(8,128)(2,1)S(1)} collective-permute-done((bf16[512,256]{1,0:T(8,128)(2,1)S(1)}, bf16[512,256]{1,0:T(8,128)(2,1)S(1)}, u32[]{:S(2)}, u32[]{:S(2)}) %collective-permute-start.19) | collective-permute-done | bytes 262176 | tf_op jit(solution)/shard_map/ppermute | solution.py:416
  83.0 2.9 %collective-permute-start.18 = (bf16[512,256]{1,0:T(8,128)(2,1)S(1)}, bf16[512,256]{1,0:T(8,128)(2,1)S(1)}, u32[]{:S(2)}, u32[]{:S(2)}) collective-permute-start(bf16[512,256]{1,0:T(8,128)(2,1)S(1)} %get-tuple-element.122), channel_id=1, source_target_pairs={{0,6},{1,7},{2,0},{3,1},{4,2},{5,3},{6,4},{7,5},{8,14},{9,15},{10,... | collective-permute-start | bytes 786440 | tf_op jit(solution)/shard_map/ppermute | solution.py:416
  85.9 0.9 final.2.refs_6_
  86.8 2.2 %collective-permute-done.13.refs_1_ = bf16[512,256]{1,0:T(8,128)(2,1)S(1)} collective-permute-done((bf16[512,256]{1,0:T(8,128)(2,1)S(1)}, bf16[512,256]{1,0:T(8,128)(2,1)S(1)}, u32[]{:S(2)}, u32[]{:S(2)}) %collective-permute-start.13) | collective-permute-done | bytes 262176 | tf_op jit(solution)/shard_map/ppermute | solution.py:416
  89.0 1.6 %collective-permute-done.18.refs_5_ = bf16[512,256]{1,0:T(8,128)(2,1)S(1)} collective-permute-done((bf16[512,256]{1,0:T(8,128)(2,1)S(1)}, bf16[512,256]{1,0:T(8,128)(2,1)S(1)}, u32[]{:S(2)}, u32[]{:S(2)}) %collective-permute-start.18) | collective-permute-done | bytes 262176 | tf_op jit(solution)/shard_map/ppermute | solution.py:416
  90.5 0.9 final.3
  (23 shorter events, 0.3 us)
Async XLA Ops:
  0.0 9.6 %copy-start = (bf16[512,2048]{1,0:T(8,128)(2,1)S(1)}, bf16[512,2048]{1,0:T(8,128)(2,1)}, u32[]{:S(2)}) copy-start(bf16[512,2048]{1,0:T(8,128)(2,1)} %w_own.7) | copy-start | bytes 6291460
  7.9 6.7 %collective-permute-start = (bf16[4,128,128]{2,1,0:T(8,128)(2,1)S(1)}, bf16[4,128,128]{2,1,0:T(8,128)(2,1)S(1)}, u32[]{:S(2)}, u32[]{:S(2)}) collective-permute-start(bf16[4,128,128]{2,1,0:T(8,128)(2,1)S(1)} %get-tuple-element.69.refs_0_), channel_id=1, source_target_pairs={{0,8},{8,0},{16,24},{24,16},{32,40},{40,32},{48,56},{56,48},{64,72... | collective-permute-start | bytes 393224 | tf_op jit(solution)/shard_map/ppermute | solution.py:429
  9.6 37.7 %collective-permute-start.7 = (bf16[512,2048]{1,0:T(8,128)(2,1)S(1)}, bf16[512,2048]{1,0:T(8,128)(2,1)S(1)}, u32[]{:S(2)}, u32[]{:S(2)}) collective-permute-start(bf16[512,2048]{1,0:T(8,128)(2,1)S(1)} %copy-done), channel_id=1, source_target_pairs={{0,1},{1,0},{2,3},{3,2},{4,5},{5,4},{6,7},{7,6},{8,9},{9,8},{10,11... | collective-permute-start | bytes 6291464 | tf_op jit(solution)/shard_map/ppermute | solution.py:413
  9.6 7.9 %copy-start.1 = (bf16[4,128,17]{1,0,2:T(4,128)(2,1)S(1)}, bf16[4,128,17]{1,0,2:T(4,128)(2,1)}, u32[]{:S(2)}) copy-start(bf16[4,128,17]{1,0,2:T(4,128)(2,1)} %param.7) | copy-start | bytes 52228
  14.7 7.2 %collective-permute-start.1 = (bf16[4,128,128]{2,1,0:T(8,128)(2,1)S(1)}, bf16[4,128,128]{2,1,0:T(8,128)(2,1)S(1)}, u32[]{:S(2)}, u32[]{:S(2)}) collective-permute-start(bf16[4,128,128]{2,1,0:T(8,128)(2,1)S(1)} %added.7.after.refs_0_), channel_id=1, source_target_pairs={{0,24},{8,16},{16,8},{24,0},{32,56},{40,48},{48,40},{56,32},{64,88... | collective-permute-start | bytes 393224 | tf_op jit(solution)/shard_map/ppermute | solution.py:429
  16.9 7.1 %collective-permute-start.3 = (bf16[4,128,128]{2,1,0:T(8,128)(2,1)S(1)}, bf16[4,128,128]{2,1,0:T(8,128)(2,1)S(1)}, u32[]{:S(2)}, u32[]{:S(2)}) collective-permute-start(bf16[4,128,128]{2,1,0:T(8,128)(2,1)S(1)} %get-tuple-element.83.refs_0_), channel_id=1, source_target_pairs={{0,8},{8,0},{16,24},{24,16},{32,40},{40,32},{48,56},{56,48},{64,72... | collective-permute-start | bytes 393224 | tf_op jit(solution)/shard_map/ppermute | solution.py:429
  21.9 6.7 %collective-permute-start.2 = (bf16[4,128,128]{2,1,0:T(8,128)(2,1)S(1)}, bf16[4,128,128]{2,1,0:T(8,128)(2,1)S(1)}, u32[]{:S(2)}, u32[]{:S(2)}) collective-permute-start(bf16[4,128,128]{2,1,0:T(8,128)(2,1)S(1)} %added.8.refs_0_), channel_id=1, source_target_pairs={{0,32},{8,40},{16,48},{24,56},{32,0},{40,8},{48,16},{56,24},{64,96... | collective-permute-start | bytes 393224 | tf_op jit(solution)/shard_map/ppermute | solution.py:429
  24.0 7.3 %collective-permute-start.5 = (bf16[4,128,128]{2,1,0:T(8,128)(2,1)S(1)}, bf16[4,128,128]{2,1,0:T(8,128)(2,1)S(1)}, u32[]{:S(2)}, u32[]{:S(2)}) collective-permute-start(bf16[4,128,128]{2,1,0:T(8,128)(2,1)S(1)} %added.9.after.refs_0_), channel_id=1, source_target_pairs={{0,24},{8,16},{16,8},{24,0},{32,56},{40,48},{48,40},{56,32},{64,88... | collective-permute-start | bytes 393224 | tf_op jit(solution)/shard_map/ppermute | solution.py:429
  28.6 6.3 %collective-permute-start.4 = (bf16[4,128,128]{2,1,0:T(8,128)(2,1)S(1)}, bf16[4,128,128]{2,1,0:T(8,128)(2,1)S(1)}, u32[]{:S(2)}, u32[]{:S(2)}) collective-permute-start(bf16[4,128,128]{2,1,0:T(8,128)(2,1)S(1)} %added.10.refs_0_), channel_id=1, source_target_pairs={{0,96},{8,104},{16,112},{24,120},{32,64},{40,72},{48,80},{56,88},{... | collective-permute-start | bytes 393224 | tf_op jit(solution)/shard_map/ppermute | solution.py:429
  31.3 3.6 %copy-start.2 = (f32[512]{0:T(512)S(1)}, f32[512]{0:T(512)}, u32[]{:S(2)}) copy-start(f32[512]{0:T(512)} %param.8) | copy-start | bytes 6148
  36.4 10.9 %collective-permute-start.6 = (bf16[1024,512]{1,0:T(8,128)(2,1)S(1)}, bf16[1024,512]{1,0:T(8,128)(2,1)S(1)}, u32[]{:S(2)}, u32[]{:S(2)}) collective-permute-start(bf16[1024,512]{1,0:T(8,128)(2,1)S(1)} %far_part.2.own.after), channel_id=1, source_target_pairs={{0,1},{1,0},{2,3},{3,2},{4,5},{5,4},{6,7},{7,6},{8,9},{9,8},{10,11... | collective-permute-start | bytes 3145736 | tf_op jit(solution)/shard_map/ppermute | solution.py:413
  36.5 5.9 %collective-permute-start.8 = (bf16[4,128,128]{2,1,0:T(8,128)(2,1)S(1)}, bf16[4,128,128]{2,1,0:T(8,128)(2,1)S(1)}, u32[]{:S(2)}, u32[]{:S(2)}) collective-permute-start(bf16[4,128,128]{2,1,0:T(8,128)(2,1)S(1)} %added.11.after.refs_0_), channel_id=1, source_target_pairs={{0,32},{8,40},{16,48},{24,56},{32,0},{40,8},{48,16},{56,24},{64,96... | collective-permute-start | bytes 393224 | tf_op jit(solution)/shard_map/ppermute | solution.py:429
  42.4 6.3 %collective-permute-start.9 = (bf16[4,128,128]{2,1,0:T(8,128)(2,1)S(1)}, bf16[4,128,128]{2,1,0:T(8,128)(2,1)S(1)}, u32[]{:S(2)}, u32[]{:S(2)}) collective-permute-start(bf16[4,128,128]{2,1,0:T(8,128)(2,1)S(1)} %added.12), channel_id=1, source_target_pairs={{0,96},{8,104},{16,112},{24,120},{32,64},{40,72},{48,80},{56,88},{... | collective-permute-start | bytes 393224 | tf_op jit(solution)/shard_map/ppermute | solution.py:429
  50.4 5.2 %collective-permute-start.10 = (bf16[1024,512]{1,0:T(8,128)(2,1)S(1)}, bf16[1024,512]{1,0:T(8,128)(2,1)S(1)}, u32[]{:S(2)}, u32[]{:S(2)}) collective-permute-start(bf16[1024,512]{1,0:T(8,128)(2,1)S(1)} %far_part.3.own), channel_id=1, source_target_pairs={{0,1},{1,0},{2,3},{3,2},{4,5},{5,4},{6,7},{7,6},{8,9},{9,8},{10,11... | collective-permute-start | bytes 3145736 | tf_op jit(solution)/shard_map/ppermute | solution.py:413
  50.5 11.2 %collective-permute-start.14 = (bf16[512,256]{1,0:T(8,128)(2,1)S(1)}, bf16[512,256]{1,0:T(8,128)(2,1)S(1)}, u32[]{:S(2)}, u32[]{:S(2)}) collective-permute-start(bf16[512,256]{1,0:T(8,128)(2,1)S(1)} %get-tuple-element.102.after), channel_id=1, source_target_pairs={{0,2},{1,3},{2,4},{3,5},{4,6},{5,7},{6,0},{7,1},{8,10},{9,11},{10,... | collective-permute-start | bytes 786440 | tf_op jit(solution)/shard_map/ppermute | solution.py:416
  52.2 9.5 %collective-permute-start.15 = (bf16[512,256]{1,0:T(8,128)(2,1)S(1)}, bf16[512,256]{1,0:T(8,128)(2,1)S(1)}, u32[]{:S(2)}, u32[]{:S(2)}) collective-permute-start(bf16[512,256]{1,0:T(8,128)(2,1)S(1)} %get-tuple-element.116), channel_id=1, source_target_pairs={{0,6},{1,7},{2,0},{3,1},{4,2},{5,3},{6,4},{7,5},{8,14},{9,15},{10,... | collective-permute-start | bytes 786440 | tf_op jit(solution)/shard_map/ppermute | solution.py:416
  56.3 10.6 %collective-permute-start.11 = (bf16[512,256]{1,0:T(8,128)(2,1)S(1)}, bf16[512,256]{1,0:T(8,128)(2,1)S(1)}, u32[]{:S(2)}, u32[]{:S(2)}) collective-permute-start(bf16[512,256]{1,0:T(8,128)(2,1)S(1)} %get-tuple-element.111), channel_id=1, source_target_pairs={{0,2},{1,3},{2,4},{3,5},{4,6},{5,7},{6,0},{7,1},{8,10},{9,11},{10,... | collective-permute-start | bytes 786440 | tf_op jit(solution)/shard_map/ppermute | solution.py:416
  57.0 10.0 %collective-permute-start.12 = (bf16[512,256]{1,0:T(8,128)(2,1)S(1)}, bf16[512,256]{1,0:T(8,128)(2,1)S(1)}, u32[]{:S(2)}, u32[]{:S(2)}) collective-permute-start(bf16[512,256]{1,0:T(8,128)(2,1)S(1)} %get-tuple-element.112), channel_id=1, source_target_pairs={{0,6},{1,7},{2,0},{3,1},{4,2},{5,3},{6,4},{7,5},{8,14},{9,15},{10,... | collective-permute-start | bytes 786440 | tf_op jit(solution)/shard_map/ppermute | solution.py:416
  61.9 24.1 %collective-permute-start.16 = (bf16[1024,256]{1,0:T(8,128)(2,1)S(1)}, bf16[1024,256]{1,0:T(8,128)(2,1)S(1)}, u32[]{:S(2)}, u32[]{:S(2)}) collective-permute-start(bf16[1024,256]{1,0:T(8,128)(2,1)S(1)} %get-tuple-element.119), channel_id=1, source_target_pairs={{0,6},{1,7},{2,0},{3,1},{4,2},{5,3},{6,4},{7,5},{8,14},{9,15},{10,... | collective-permute-start | bytes 1572872 | tf_op jit(solution)/shard_map/ppermute | solution.py:416
  63.7 22.2 %collective-permute-start.17 = (bf16[1024,256]{1,0:T(8,128)(2,1)S(1)}, bf16[1024,256]{1,0:T(8,128)(2,1)S(1)}, u32[]{:S(2)}, u32[]{:S(2)}) collective-permute-start(bf16[1024,256]{1,0:T(8,128)(2,1)S(1)} %get-tuple-element.121), channel_id=1, source_target_pairs={{0,2},{1,3},{2,4},{3,5},{4,6},{5,7},{6,0},{7,1},{8,10},{9,11},{10,... | collective-permute-start | bytes 1572872 | tf_op jit(solution)/shard_map/ppermute | solution.py:416
  64.0 19.0 %collective-permute-start.19 = (bf16[512,256]{1,0:T(8,128)(2,1)S(1)}, bf16[512,256]{1,0:T(8,128)(2,1)S(1)}, u32[]{:S(2)}, u32[]{:S(2)}) collective-permute-start(bf16[512,256]{1,0:T(8,128)(2,1)S(1)} %get-tuple-element.124), channel_id=1, source_target_pairs={{0,6},{1,7},{2,0},{3,1},{4,2},{5,3},{6,4},{7,5},{8,14},{9,15},{10,... | collective-permute-start | bytes 786440 | tf_op jit(solution)/shard_map/ppermute | solution.py:416
  67.0 18.9 %collective-permute-start.20 = (bf16[512,256]{1,0:T(8,128)(2,1)S(1)}, bf16[512,256]{1,0:T(8,128)(2,1)S(1)}, u32[]{:S(2)}, u32[]{:S(2)}) collective-permute-start(bf16[512,256]{1,0:T(8,128)(2,1)S(1)} %get-tuple-element.126), channel_id=1, source_target_pairs={{0,2},{1,3},{2,4},{3,5},{4,6},{5,7},{6,0},{7,1},{8,10},{9,11},{10,... | collective-permute-start | bytes 786440 | tf_op jit(solution)/shard_map/ppermute | solution.py:416
  67.1 21.9 %collective-permute-start.13 = (bf16[512,256]{1,0:T(8,128)(2,1)S(1)}, bf16[512,256]{1,0:T(8,128)(2,1)S(1)}, u32[]{:S(2)}, u32[]{:S(2)}) collective-permute-start(bf16[512,256]{1,0:T(8,128)(2,1)S(1)} %get-tuple-element.113), channel_id=1, source_target_pairs={{0,2},{1,3},{2,4},{3,5},{4,6},{5,7},{6,0},{7,1},{8,10},{9,11},{10,... | collective-permute-start | bytes 786440 | tf_op jit(solution)/shard_map/ppermute | solution.py:416
  83.0 7.6 %collective-permute-start.18 = (bf16[512,256]{1,0:T(8,128)(2,1)S(1)}, bf16[512,256]{1,0:T(8,128)(2,1)S(1)}, u32[]{:S(2)}, u32[]{:S(2)}) collective-permute-start(bf16[512,256]{1,0:T(8,128)(2,1)S(1)} %get-tuple-element.122), channel_id=1, source_target_pairs={{0,6},{1,7},{2,0},{3,1},{4,2},{5,3},{6,4},{7,5},{8,14},{9,15},{10,... | collective-permute-start | bytes 786440 | tf_op jit(solution)/shard_map/ppermute | solution.py:416

commit v3 on v2

--- a/solution.py
+++ b/solution.py
@@ -32,13 +32,17 @@
     return sum((number >= 2**j).astype(jnp.int32) for j in range(4))
 
 
-def key_value_block(heads, dim, block, rows, wk, wv, k_out, vt_out, chunk_out, total, keys=None):
+def key_value_block(
+    heads, dim, block, rows, wk, wv, k_out, vt_out, chunk_out, total, keys=None, values=None
+):
     at = slice(block * BLOCK, (block + 1) * BLOCK)
     if keys is None:
         keys = dot(rows, wk[...])
     keys = keys.astype(BF16)
     k_out[at] = keys
-    values = dot(rows, wv[...]).astype(BF16)
+    if values is None:
+        values = dot(rows, wv[...])
+    values = values.astype(BF16)
     for head in range(heads):
         cols = slice(head * dim, (head + 1) * dim)
         turned = values[:, cols].T
@@ -54,41 +58,50 @@
 
 def first_kernel(heads, dim, tok_in, w_in, k_out, vt_out, chunk_out, total_out, tok, wq, wk, wv, total, sems):
     depth = tok.shape[1]
-    part = depth // 2
-    blocks = k_out.shape[0] // BLOCK
-    head_rows = pl.ds(0, BLOCK)
+    parts = 4
+    part = depth // parts
+    rows = k_out.shape[0]
+    blocks = rows // BLOCK
+    opening = pl.ds(0, BLOCK)
     pairs = []
-    for j in range(2):
+    for j in range(parts):
         at = pl.ds(j * part, part)
         pairs.append((w_in.at[1, at], wk.at[at]))
-        pairs.append((tok_in.at[head_rows, at], tok.at[head_rows, at]))
-    pairs.append((w_in.at[2], wv))
-    rows = k_out.shape[0]
+        pairs.append((tok_in.at[opening, at], tok.at[opening, at]))
+    for j in range(parts):
+        at = pl.ds(j * part, part)
+        pairs.append((w_in.at[2, at], wv.at[at]))
     for start, stop in ((BLOCK, rows), (rows, tok.shape[0])):
         at = pl.ds(start, stop - start)
         pairs.append((tok_in.at[at], tok.at[at]))
     pairs.append((w_in.at[0], wq))
     copies = [pltpu.make_async_copy(*pair, sems.at[j]) for j, pair in enumerate(pairs)]
-    for copy in copies[:4]:
+    later = copies[2 * parts :]
+    for copy in copies[: 2 * parts]:
         copy.start()
-    keys = None
-    for j in range(2):
+    keys = values = None
+    for j in range(parts):
         copies[2 * j].wait()
         copies[2 * j + 1].wait()
-        copies[4 + j].start()
+        later[j].start()
         at = slice(j * part, (j + 1) * part)
         term = dot(tok[:BLOCK, at], wk[at])
         keys = term if keys is None else keys + term
-    copies[4].wait()
-    copies[6].start()
-    copies[7].start()
+    later[parts].start()
+    for j in range(parts):
+        later[j].wait()
+        at = slice(j * part, (j + 1) * part)
+        term = dot(tok[:BLOCK, at], wv[at])
+        values = term if values is None else values + term
+    later[parts + 1].start()
+    later[parts + 2].start()
     outs = (wk, wv, k_out, vt_out, chunk_out, total)
-    key_value_block(heads, dim, 0, tok[:BLOCK], *outs, keys)
-    copies[5].wait()
+    key_value_block(heads, dim, 0, tok[:BLOCK], *outs, keys, values)
+    later[parts].wait()
     for block in range(1, blocks):
         key_value_block(heads, dim, block, tok[block * BLOCK : (block + 1) * BLOCK], *outs)
-    copies[6].wait()
-    copies[7].wait()
+    later[parts + 1].wait()
+    later[parts + 2].wait()
     total_out[...] = total[...].astype(BF16)
 
 
@@ -114,7 +127,7 @@
     if first:
         shapes.append(jax.ShapeDtypeStruct(args[0].shape, BF16))
         shapes += [jax.ShapeDtypeStruct((depth, width), BF16)] * 3
-        scratch.append(pltpu.SemaphoreType.DMA((8,)))
+        scratch.append(pltpu.SemaphoreType.DMA((15,)))
     return pl.pallas_call(
         functools.partial(first_kernel if first else second_kernel, heads, dim),
         in_specs=[pl.BlockSpec(memory_space=pltpu.HBM)] * 2 if first else [vmem] * 3,

time: 92.3 us -> 92 us (level)
  no operation moved by 1% of the time
where the time goes in v3:
time: 92 us; the launch traced here: 91.3 us
  Pallas kernels  32 us (35%)
  starting transfers between devices  31.1 us (34%)
  waiting for transfers between devices  27.8 us (30%)
    ppermute x10, waiting for transfers between devices, over_ring(): lax.ppermute(value, 'head', [(i, (i + 2 * shift) % head_count) for i in r...  18 us
    ppermute x10, starting transfers between devices, over_ring(): lax.ppermute(value, 'head', [(i, (i + 2 * shift) % head_count) for i in r...  16.5 us
    ppermute x8, starting transfers between devices, over_ctx(): return lax.ppermute(value, 'ctx', [(i, i ^ mask) for i in range(ctx_count)])  14.4 us
    pallas_call x2, Pallas kernels, key_value(): pl.pallas_call(functools.partial(first_kernel if first else second_kernel...  12.6 us
    ppermute x8, waiting for transfers between devices, over_ctx(): return lax.ppermute(value, 'ctx', [(i, i ^ mask) for i in range(ctx_count)])  9.76 us
    pallas_call x4, Pallas kernels, near_part(): pl.pallas_call(functools.partial(near_kernel, heads, dim, half, step), in...  8.88 us
    pallas_call x4, Pallas kernels, project(): pl.pallas_call(functools.partial(project_kernel, feats, ring, shifts), in...  5.04 us
    pallas_call x2, Pallas kernels, far_part(): pl.pallas_call(functools.partial(far_kernel, heads, dim, level0, count, c...  3.2 us
  transfers between devices with their start and end apart: 21, of which 7 were waited for; matrix products, arithmetic and copies ran while one was open for 0% of the time, Pallas kernels for 24%

profile of v3, /device:TPU:0, one launch (start us, length us, event | category | flops | bytes accessed | tf_op | source)
XLA Modules:
  0.0 91.3 jit_solution(2836416400773155285)
XLA Ops:
  0.0 7.6 %key_value.2 = (bf16[1024,512]{1,0:T(8,128)(2,1)S(1)}, bf16[2,512,512]{2,1,0:T(8,128)(2,1)S(1)}, bf16[4,4,128,128]{3,2,1,0:T(8,128)(2,1)S(1)}, bf16[4,128,128]{2...) custom-call(bf16[2048,2048]{1,0:T(8,128)(2,1)} %tok_in, ...), custom_call_target="tpu_custom_call" | custom-call | flops 4294967296 | bytes 14680064 | tf_op jit(solution)/shard_map/key_value/pallas_call | solution.py:131
  7.6 1.7 %collective-permute-start = (bf16[4,128,128]{2,1,0:T(8,128)(2,1)S(1)}, bf16[4,128,128]{2,1,0:T(8,128)(2,1)S(1)}, u32[]{:S(2)}, u32[]{:S(2)}) collective-permute-start(bf16[4,128,128]{2,1,0:T(8,128)(2,1)S(1)} %get-tuple-element.69.refs_0_), channel_id=1, source_target_pairs={{0,8},{8,0},{16,24},{24,16},{32,40},{40,32},{48,56},{56,48},{64,72... | collective-permute-start | bytes 393224 | tf_op jit(solution)/shard_map/ppermute | solution.py:442
  9.3 0.0 collective-permute-start.7
  9.3 5.0 %key_value.3 = (bf16[1024,512]{1,0:T(8,128)(2,1)S(1)}, bf16[2,512,512]{2,1,0:T(8,128)(2,1)S(1)}, bf16[4,4,128,128]{3,2,1,0:T(8,128)(2,1)S(1)}, bf16[4,128,128]{2,1,0:T(8,128)(2,1)S(1)}) custom-call(bf16[2048,2048]{1,0:T(8,128)(2,1)S(1)} %get-tuple-element.70.tok, bf16[2048,512]{1,0:T(8,128)(2,1)S(1)} %get-tuple-element.71.wk, ...), custom_call_target="tpu_custom_call" | custom-call | flops 4294967296 | bytes 14680064 | tf_op jit(solution)/shard_map/key_value/pallas_call | solution.py:131
  14.3 0.0 collective-permute-done.refs_1_.refs_6_
  14.4 2.2 %collective-permute-start.1 = (bf16[4,128,128]{2,1,0:T(8,128)(2,1)S(1)}, bf16[4,128,128]{2,1,0:T(8,128)(2,1)S(1)}, u32[]{:S(2)}, u32[]{:S(2)}) collective-permute-start(bf16[4,128,128]{2,1,0:T(8,128)(2,1)S(1)} %added.7.after.refs_0_), channel_id=1, source_target_pairs={{0,24},{8,16},{16,8},{24,0},{32,56},{40,48},{48,40},{56,32},{64,88... | collective-permute-start | bytes 393224 | tf_op jit(solution)/shard_map/ppermute | solution.py:442
  16.6 0.6 collective-permute-start.3
  17.1 2.2 %near_part.4 = (f32[512,512]{1,0:T(8,128)S(1)}, bf16[512,512]{1,0:T(8,128)(2,1)S(1)}, f32[68,512]{1,0:T(8,128)S(1)}) custom-call(bf16[2048,2048]{1,0:T(8,128)(2,1)S(1)} %get-tuple-element.70.tok, bf16[2048,512]{1,0:T(8,128)(2,1)S(1)} %get-tuple-element.75.wq, bf16[1024,512]{1,0:T(8,128)(2,1)S(1)} %get-tuple-element.76.keys, ...), custom_call_target="tpu_custom_call" | custom-call | flops 2147483648 | bytes 14680064 | tf_op jit(solution)/shard_map/near_part/pallas_call | solution.py:259
  19.3 2.2 %collective-permute-done.1.refs_1_.refs_7_ = bf16[4,128,128]{2,1,0:T(8,128)(2,1)S(1)} collective-permute-done((bf16[4,128,128]{2,1,0:T(8,128)(2,1)S(1)}, bf16[4,128,128]{2,1,0:T(8,128)(2,1)S(1)}, u32[]{:S(2)}, u32[]{:S(2)}) %collective-permute-start.1) | collective-permute-done | bytes 131104 | tf_op jit(solution)/shard_map/ppermute | solution.py:442
  21.6 2.0 %collective-permute-start.2 = (bf16[4,128,128]{2,1,0:T(8,128)(2,1)S(1)}, bf16[4,128,128]{2,1,0:T(8,128)(2,1)S(1)}, u32[]{:S(2)}, u32[]{:S(2)}) collective-permute-start(bf16[4,128,128]{2,1,0:T(8,128)(2,1)S(1)} %added.8.refs_0_), channel_id=1, source_target_pairs={{0,32},{8,40},{16,48},{24,56},{32,0},{40,8},{48,16},{56,24},{64,96... | collective-permute-start | bytes 393224 | tf_op jit(solution)/shard_map/ppermute | solution.py:442
  23.6 0.0 collective-permute-done.3.refs_1_.refs_6_
  23.6 2.4 %collective-permute-start.5 = (bf16[4,128,128]{2,1,0:T(8,128)(2,1)S(1)}, bf16[4,128,128]{2,1,0:T(8,128)(2,1)S(1)}, u32[]{:S(2)}, u32[]{:S(2)}) collective-permute-start(bf16[4,128,128]{2,1,0:T(8,128)(2,1)S(1)} %added.9.after.refs_0_), channel_id=1, source_target_pairs={{0,24},{8,16},{16,8},{24,0},{32,56},{40,48},{48,40},{56,32},{64,88... | collective-permute-start | bytes 393224 | tf_op jit(solution)/shard_map/ppermute | solution.py:442
  26.0 2.3 %near_part.5 = (f32[512,512]{1,0:T(8,128)S(1)}, bf16[512,512]{1,0:T(8,128)(2,1)S(1)}, f32[68,512]{1,0:T(8,128)S(1)}) custom-call(bf16[2048,2048]{1,0:T(8,128)(2,1)S(1)} %get-tuple-element.70.tok, bf16[2048,512]{1,0:T(8,128)(2,1)S(1)} %get-tuple-element.75.wq, bf16[1024,512]{1,0:T(8,128)(2,1)S(1)} %get-tuple-element.76.keys, ...), custom_call_target="tpu_custom_call" | custom-call | flops 2147483648 | bytes 14680064 | tf_op jit(solution)/shard_map/near_part/pallas_call | solution.py:259
  28.3 0.0 collective-permute-done.2.refs_1_.refs_8_
  28.3 2.6 %collective-permute-start.4 = (bf16[4,128,128]{2,1,0:T(8,128)(2,1)S(1)}, bf16[4,128,128]{2,1,0:T(8,128)(2,1)S(1)}, u32[]{:S(2)}, u32[]{:S(2)}) collective-permute-start(bf16[4,128,128]{2,1,0:T(8,128)(2,1)S(1)} %added.10.refs_0_), channel_id=1, source_target_pairs={{0,96},{8,104},{16,112},{24,120},{32,64},{40,72},{48,80},{56,88},{... | collective-permute-start | bytes 393224 | tf_op jit(solution)/shard_map/ppermute | solution.py:442
  31.0 0.0 copy-start.2
  31.0 2.2 %near_part.6 = (f32[512,512]{1,0:T(8,128)S(1)}, bf16[512,512]{1,0:T(8,128)(2,1)S(1)}, f32[68,512]{1,0:T(8,128)S(1)}) custom-call(bf16[2048,2048]{1,0:T(8,128)(2,1)S(1)} %get-tuple-element.70.tok, bf16[2048,512]{1,0:T(8,128)(2,1)S(1)} %get-tuple-element.75.wq, bf16[1024,512]{1,0:T(8,128)(2,1)S(1)} %get-tuple-element.88.keys, ...), custom_call_target="tpu_custom_call" | custom-call | flops 2147483648 | bytes 14680064 | tf_op jit(solution)/shard_map/near_part/pallas_call | solution.py:259
  33.2 1.4 %collective-permute-done.4.refs_9_.refs_1_ = bf16[4,128,128]{2,1,0:T(8,128)(2,1)S(1)} collective-permute-done((bf16[4,128,128]{2,1,0:T(8,128)(2,1)S(1)}, bf16[4,128,128]{2,1,0:T(8,128)(2,1)S(1)}, u32[]{:S(2)}, u32[]{:S(2)}) %collective-permute-start.4) | collective-permute-done | bytes 131104 | tf_op jit(solution)/shard_map/ppermute | solution.py:442
  34.6 1.5 %far_part.2.own.after = bf16[1024,512]{1,0:T(8,128)(2,1)S(1)} custom-call(s32[1]{0:T(128)} %bitcast.device, f32[68,512]{1,0:T(8,128)S(1)} %get-tuple-element.94.after.refs_2_, f32[1,512]{1,0:T(1,128)S(1)} %bitcast.9, f32[512,512]{1,0:T(8,128)S(1)} %get-tuple-element.95.refs_0_, bf16[512,512]{1,0:T(8,128)(2,1)S(1)} %get-tuple-element.96.refs_1_, ...), custom_call_target="tpu_custom_call" | custom-call | flops 536870912 | bytes 5242880 | tf_op jit(solution)/shard_map/far_part/pallas_call | solution.py:312
  36.0 0.1 collective-permute-start.6
  36.1 0.4 collective-permute-start.8
  36.5 5.5 %collective-permute-done.8.refs_1_.refs_8_ = bf16[4,128,128]{2,1,0:T(8,128)(2,1)S(1)} collective-permute-done((bf16[4,128,128]{2,1,0:T(8,128)(2,1)S(1)}, bf16[4,128,128]{2,1,0:T(8,128)(2,1)S(1)}, u32[]{:S(2)}, u32[]{:S(2)}) %collective-permute-start.8) | collective-permute-done | bytes 131104 | tf_op jit(solution)/shard_map/ppermute | solution.py:442
  42.1 2.6 %collective-permute-start.9 = (bf16[4,128,128]{2,1,0:T(8,128)(2,1)S(1)}, bf16[4,128,128]{2,1,0:T(8,128)(2,1)S(1)}, u32[]{:S(2)}, u32[]{:S(2)}) collective-permute-start(bf16[4,128,128]{2,1,0:T(8,128)(2,1)S(1)} %added.12), channel_id=1, source_target_pairs={{0,96},{8,104},{16,112},{24,120},{32,64},{40,72},{48,80},{56,88},{... | collective-permute-start | bytes 393224 | tf_op jit(solution)/shard_map/ppermute | solution.py:442
  44.7 2.3 %near_part.7 = (f32[512,512]{1,0:T(8,128)S(1)}, bf16[512,512]{1,0:T(8,128)(2,1)S(1)}, f32[68,512]{1,0:T(8,128)S(1)}) custom-call(bf16[2048,2048]{1,0:T(8,128)(2,1)S(1)} %get-tuple-element.70.tok, bf16[2048,512]{1,0:T(8,128)(2,1)S(1)} %get-tuple-element.75.wq, bf16[1024,512]{1,0:T(8,128)(2,1)S(1)} %get-tuple-element.88.keys, ...), custom_call_target="tpu_custom_call" | custom-call | flops 2147483648 | bytes 14680064 | tf_op jit(solution)/shard_map/near_part/pallas_call | solution.py:259
  47.0 0.0 collective-permute-done.7.w_peer
  47.0 0.7 project.4
  47.7 0.6 collective-permute-done.9.refs_9_
  48.3 1.7 %far_part.3.own = bf16[1024,512]{1,0:T(8,128)(2,1)S(1)} custom-call(s32[1]{0:T(128)} %bitcast.device, bf16[512,256]{1,0:T(8,128)(2,1)S(1)} %get-tuple-element.102.after, f32[1,512]{1,0:T(1,128)S(1)} %bitcast.10, f32[512,512]{1,0:T(8,128)S(1)} %get-tuple-element.103.refs_0_, bf16[512,512]{1,0:T(8,128)(2,1)S(1)} %get-tuple-element.104.refs_1_, ...), custom_call_target="tpu_custom_call" | custom-call | flops 671088640 | bytes 5242880 | tf_op jit(solution)/shard_map/far_part/pallas_call | solution.py:312
  50.1 0.1 collective-permute-start.10
  50.2 1.6 %collective-permute-start.14 = (bf16[512,256]{1,0:T(8,128)(2,1)S(1)}, bf16[512,256]{1,0:T(8,128)(2,1)S(1)}, u32[]{:S(2)}, u32[]{:S(2)}) collective-permute-start(bf16[512,256]{1,0:T(8,128)(2,1)S(1)} %get-tuple-element.102.after), channel_id=1, source_target_pairs={{0,2},{1,3},{2,4},{3,5},{4,6},{5,7},{6,0},{7,1},{8,10},{9,11},{10,... | collective-permute-start | bytes 786440 | tf_op jit(solution)/shard_map/ppermute | solution.py:429
  51.8 1.7 %collective-permute-start.15 = (bf16[512,256]{1,0:T(8,128)(2,1)S(1)}, bf16[512,256]{1,0:T(8,128)(2,1)S(1)}, u32[]{:S(2)}, u32[]{:S(2)}) collective-permute-start(bf16[512,256]{1,0:T(8,128)(2,1)S(1)} %get-tuple-element.116), channel_id=1, source_target_pairs={{0,6},{1,7},{2,0},{3,1},{4,2},{5,3},{6,4},{7,5},{8,14},{9,15},{10,... | collective-permute-start | bytes 786440 | tf_op jit(solution)/shard_map/ppermute | solution.py:429
  53.5 1.8 %project.7 = (bf16[512,256]{1,0:T(8,128)(2,1)S(1)}, bf16[512,256]{1,0:T(8,128)(2,1)S(1)}, bf16[512,256]{1,0:T(8,128)(2,1)S(1)}, bf16[512,256]{1,0:T(8,128)(2,1)S...) custom-call(s32[1]{0:T(128)} %bitcast.1.group, bf16[1024,512]{1,0:T(8,128)(2,1)S(1)} %far_part.2.own.after, ...), custom_call_target="tpu_custom_call" | custom-call | flops 1610612736 | bytes 4194304 | tf_op jit(solution)/shard_map/project/pallas_call | solution.py:341
  55.3 0.7 project.6
  56.0 0.7 collective-permute-start.11
  56.7 2.9 %collective-permute-start.12 = (bf16[512,256]{1,0:T(8,128)(2,1)S(1)}, bf16[512,256]{1,0:T(8,128)(2,1)S(1)}, u32[]{:S(2)}, u32[]{:S(2)}) collective-permute-start(bf16[512,256]{1,0:T(8,128)(2,1)S(1)} %get-tuple-element.112), channel_id=1, source_target_pairs={{0,6},{1,7},{2,0},{3,1},{4,2},{5,3},{6,4},{7,5},{8,14},{9,15},{10,... | collective-permute-start | bytes 786440 | tf_op jit(solution)/shard_map/ppermute | solution.py:429
  59.5 1.8 %project.5 = (bf16[512,256]{1,0:T(8,128)(2,1)S(1)}, bf16[512,256]{1,0:T(8,128)(2,1)S(1)}, bf16[512,256]{1,0:T(8,128)(2,1)S(1)}, bf16[512,256]{1,0:T(8,128)(2,1)S...) custom-call(s32[1]{0:T(128)} %bitcast.1.group, bf16[1024,512]{1,0:T(8,128)(2,1)S(1)} %far_part.3.own, ...), custom_call_target="tpu_custom_call" | custom-call | flops 1610612736 | bytes 4194304 | tf_op jit(solution)/shard_map/project/pallas_call | solution.py:341
  61.4 0.1 relay.3
  61.5 1.9 %collective-permute-start.16 = (bf16[1024,256]{1,0:T(8,128)(2,1)S(1)}, bf16[1024,256]{1,0:T(8,128)(2,1)S(1)}, u32[]{:S(2)}, u32[]{:S(2)}) collective-permute-start(bf16[1024,256]{1,0:T(8,128)(2,1)S(1)} %get-tuple-element.119), channel_id=1, source_target_pairs={{0,6},{1,7},{2,0},{3,1},{4,2},{5,3},{6,4},{7,5},{8,14},{9,15},{10,... | collective-permute-start | bytes 1572872 | tf_op jit(solution)/shard_map/ppermute | solution.py:429
  63.4 0.2 collective-permute-start.17
  63.6 3.0 %collective-permute-start.19 = (bf16[512,256]{1,0:T(8,128)(2,1)S(1)}, bf16[512,256]{1,0:T(8,128)(2,1)S(1)}, u32[]{:S(2)}, u32[]{:S(2)}) collective-permute-start(bf16[512,256]{1,0:T(8,128)(2,1)S(1)} %get-tuple-element.124), channel_id=1, source_target_pairs={{0,6},{1,7},{2,0},{3,1},{4,2},{5,3},{6,4},{7,5},{8,14},{9,15},{10,... | collective-permute-start | bytes 786440 | tf_op jit(solution)/shard_map/ppermute | solution.py:429
  66.7 0.1 relay.2
  66.8 1.6 %collective-permute-start.13 = (bf16[512,256]{1,0:T(8,128)(2,1)S(1)}, bf16[512,256]{1,0:T(8,128)(2,1)S(1)}, u32[]{:S(2)}, u32[]{:S(2)}) collective-permute-start(bf16[512,256]{1,0:T(8,128)(2,1)S(1)} %get-tuple-element.113), channel_id=1, source_target_pairs={{0,2},{1,3},{2,4},{3,5},{4,6},{5,7},{6,0},{7,1},{8,10},{9,11},{10,... | collective-permute-start | bytes 786440 | tf_op jit(solution)/shard_map/ppermute | solution.py:429
  68.4 14.3 %collective-permute-done.19.refs_2_ = bf16[512,256]{1,0:T(8,128)(2,1)S(1)} collective-permute-done((bf16[512,256]{1,0:T(8,128)(2,1)S(1)}, bf16[512,256]{1,0:T(8,128)(2,1)S(1)}, u32[]{:S(2)}, u32[]{:S(2)}) %collective-permute-start.19) | collective-permute-done | bytes 262176 | tf_op jit(solution)/shard_map/ppermute | solution.py:429
  82.7 2.9 %collective-permute-start.18 = (bf16[512,256]{1,0:T(8,128)(2,1)S(1)}, bf16[512,256]{1,0:T(8,128)(2,1)S(1)}, u32[]{:S(2)}, u32[]{:S(2)}) collective-permute-start(bf16[512,256]{1,0:T(8,128)(2,1)S(1)} %get-tuple-element.122), channel_id=1, source_target_pairs={{0,6},{1,7},{2,0},{3,1},{4,2},{5,3},{6,4},{7,5},{8,14},{9,15},{10,... | collective-permute-start | bytes 786440 | tf_op jit(solution)/shard_map/ppermute | solution.py:429
  85.6 0.9 final.2.refs_6_
  86.5 2.2 %collective-permute-done.13.refs_1_ = bf16[512,256]{1,0:T(8,128)(2,1)S(1)} collective-permute-done((bf16[512,256]{1,0:T(8,128)(2,1)S(1)}, bf16[512,256]{1,0:T(8,128)(2,1)S(1)}, u32[]{:S(2)}, u32[]{:S(2)}) %collective-permute-start.13) | collective-permute-done | bytes 262176 | tf_op jit(solution)/shard_map/ppermute | solution.py:429
  88.7 1.6 %collective-permute-done.18.refs_5_ = bf16[512,256]{1,0:T(8,128)(2,1)S(1)} collective-permute-done((bf16[512,256]{1,0:T(8,128)(2,1)S(1)}, bf16[512,256]{1,0:T(8,128)(2,1)S(1)}, u32[]{:S(2)}, u32[]{:S(2)}) %collective-permute-start.18) | collective-permute-done | bytes 262176 | tf_op jit(solution)/shard_map/ppermute | solution.py:429
  90.2 0.9 final.3
  (23 shorter events, 0.3 us)
Async XLA Ops:
  0.0 9.3 %copy-start = (bf16[512,2048]{1,0:T(8,128)(2,1)S(1)}, bf16[512,2048]{1,0:T(8,128)(2,1)}, u32[]{:S(2)}) copy-start(bf16[512,2048]{1,0:T(8,128)(2,1)} %w_own.7) | copy-start | bytes 6291460
  7.6 6.7 %collective-permute-start = (bf16[4,128,128]{2,1,0:T(8,128)(2,1)S(1)}, bf16[4,128,128]{2,1,0:T(8,128)(2,1)S(1)}, u32[]{:S(2)}, u32[]{:S(2)}) collective-permute-start(bf16[4,128,128]{2,1,0:T(8,128)(2,1)S(1)} %get-tuple-element.69.refs_0_), channel_id=1, source_target_pairs={{0,8},{8,0},{16,24},{24,16},{32,40},{40,32},{48,56},{56,48},{64,72... | collective-permute-start | bytes 393224 | tf_op jit(solution)/shard_map/ppermute | solution.py:442
  9.3 37.7 %collective-permute-start.7 = (bf16[512,2048]{1,0:T(8,128)(2,1)S(1)}, bf16[512,2048]{1,0:T(8,128)(2,1)S(1)}, u32[]{:S(2)}, u32[]{:S(2)}) collective-permute-start(bf16[512,2048]{1,0:T(8,128)(2,1)S(1)} %copy-done), channel_id=1, source_target_pairs={{0,1},{1,0},{2,3},{3,2},{4,5},{5,4},{6,7},{7,6},{8,9},{9,8},{10,11... | collective-permute-start | bytes 6291464 | tf_op jit(solution)/shard_map/ppermute | solution.py:426
  9.3 7.9 %copy-start.1 = (bf16[4,128,17]{1,0,2:T(4,128)(2,1)S(1)}, bf16[4,128,17]{1,0,2:T(4,128)(2,1)}, u32[]{:S(2)}) copy-start(bf16[4,128,17]{1,0,2:T(4,128)(2,1)} %param.7) | copy-start | bytes 52228
  14.4 7.2 %collective-permute-start.1 = (bf16[4,128,128]{2,1,0:T(8,128)(2,1)S(1)}, bf16[4,128,128]{2,1,0:T(8,128)(2,1)S(1)}, u32[]{:S(2)}, u32[]{:S(2)}) collective-permute-start(bf16[4,128,128]{2,1,0:T(8,128)(2,1)S(1)} %added.7.after.refs_0_), channel_id=1, source_target_pairs={{0,24},{8,16},{16,8},{24,0},{32,56},{40,48},{48,40},{56,32},{64,88... | collective-permute-start | bytes 393224 | tf_op jit(solution)/shard_map/ppermute | solution.py:442
  16.6 7.1 %collective-permute-start.3 = (bf16[4,128,128]{2,1,0:T(8,128)(2,1)S(1)}, bf16[4,128,128]{2,1,0:T(8,128)(2,1)S(1)}, u32[]{:S(2)}, u32[]{:S(2)}) collective-permute-start(bf16[4,128,128]{2,1,0:T(8,128)(2,1)S(1)} %get-tuple-element.83.refs_0_), channel_id=1, source_target_pairs={{0,8},{8,0},{16,24},{24,16},{32,40},{40,32},{48,56},{56,48},{64,72... | collective-permute-start | bytes 393224 | tf_op jit(solution)/shard_map/ppermute | solution.py:442
  21.6 6.7 %collective-permute-start.2 = (bf16[4,128,128]{2,1,0:T(8,128)(2,1)S(1)}, bf16[4,128,128]{2,1,0:T(8,128)(2,1)S(1)}, u32[]{:S(2)}, u32[]{:S(2)}) collective-permute-start(bf16[4,128,128]{2,1,0:T(8,128)(2,1)S(1)} %added.8.refs_0_), channel_id=1, source_target_pairs={{0,32},{8,40},{16,48},{24,56},{32,0},{40,8},{48,16},{56,24},{64,96... | collective-permute-start | bytes 393224 | tf_op jit(solution)/shard_map/ppermute | solution.py:442
  23.6 7.3 %collective-permute-start.5 = (bf16[4,128,128]{2,1,0:T(8,128)(2,1)S(1)}, bf16[4,128,128]{2,1,0:T(8,128)(2,1)S(1)}, u32[]{:S(2)}, u32[]{:S(2)}) collective-permute-start(bf16[4,128,128]{2,1,0:T(8,128)(2,1)S(1)} %added.9.after.refs_0_), channel_id=1, source_target_pairs={{0,24},{8,16},{16,8},{24,0},{32,56},{40,48},{48,40},{56,32},{64,88... | collective-permute-start | bytes 393224 | tf_op jit(solution)/shard_map/ppermute | solution.py:442
  28.3 6.3 %collective-permute-start.4 = (bf16[4,128,128]{2,1,0:T(8,128)(2,1)S(1)}, bf16[4,128,128]{2,1,0:T(8,128)(2,1)S(1)}, u32[]{:S(2)}, u32[]{:S(2)}) collective-permute-start(bf16[4,128,128]{2,1,0:T(8,128)(2,1)S(1)} %added.10.refs_0_), channel_id=1, source_target_pairs={{0,96},{8,104},{16,112},{24,120},{32,64},{40,72},{48,80},{56,88},{... | collective-permute-start | bytes 393224 | tf_op jit(solution)/shard_map/ppermute | solution.py:442
  31.0 3.6 %copy-start.2 = (f32[512]{0:T(512)S(1)}, f32[512]{0:T(512)}, u32[]{:S(2)}) copy-start(f32[512]{0:T(512)} %param.8) | copy-start | bytes 6148
  36.0 10.9 %collective-permute-start.6 = (bf16[1024,512]{1,0:T(8,128)(2,1)S(1)}, bf16[1024,512]{1,0:T(8,128)(2,1)S(1)}, u32[]{:S(2)}, u32[]{:S(2)}) collective-permute-start(bf16[1024,512]{1,0:T(8,128)(2,1)S(1)} %far_part.2.own.after), channel_id=1, source_target_pairs={{0,1},{1,0},{2,3},{3,2},{4,5},{5,4},{6,7},{7,6},{8,9},{9,8},{10,11... | collective-permute-start | bytes 3145736 | tf_op jit(solution)/shard_map/ppermute | solution.py:426
  36.1 5.9 %collective-permute-start.8 = (bf16[4,128,128]{2,1,0:T(8,128)(2,1)S(1)}, bf16[4,128,128]{2,1,0:T(8,128)(2,1)S(1)}, u32[]{:S(2)}, u32[]{:S(2)}) collective-permute-start(bf16[4,128,128]{2,1,0:T(8,128)(2,1)S(1)} %added.11.after.refs_0_), channel_id=1, source_target_pairs={{0,32},{8,40},{16,48},{24,56},{32,0},{40,8},{48,16},{56,24},{64,96... | collective-permute-start | bytes 393224 | tf_op jit(solution)/shard_map/ppermute | solution.py:442
  42.1 6.3 %collective-permute-start.9 = (bf16[4,128,128]{2,1,0:T(8,128)(2,1)S(1)}, bf16[4,128,128]{2,1,0:T(8,128)(2,1)S(1)}, u32[]{:S(2)}, u32[]{:S(2)}) collective-permute-start(bf16[4,128,128]{2,1,0:T(8,128)(2,1)S(1)} %added.12), channel_id=1, source_target_pairs={{0,96},{8,104},{16,112},{24,120},{32,64},{40,72},{48,80},{56,88},{... | collective-permute-start | bytes 393224 | tf_op jit(solution)/shard_map/ppermute | solution.py:442
  50.1 5.2 %collective-permute-start.10 = (bf16[1024,512]{1,0:T(8,128)(2,1)S(1)}, bf16[1024,512]{1,0:T(8,128)(2,1)S(1)}, u32[]{:S(2)}, u32[]{:S(2)}) collective-permute-start(bf16[1024,512]{1,0:T(8,128)(2,1)S(1)} %far_part.3.own), channel_id=1, source_target_pairs={{0,1},{1,0},{2,3},{3,2},{4,5},{5,4},{6,7},{7,6},{8,9},{9,8},{10,11... | collective-permute-start | bytes 3145736 | tf_op jit(solution)/shard_map/ppermute | solution.py:426
  50.2 11.2 %collective-permute-start.14 = (bf16[512,256]{1,0:T(8,128)(2,1)S(1)}, bf16[512,256]{1,0:T(8,128)(2,1)S(1)}, u32[]{:S(2)}, u32[]{:S(2)}) collective-permute-start(bf16[512,256]{1,0:T(8,128)(2,1)S(1)} %get-tuple-element.102.after), channel_id=1, source_target_pairs={{0,2},{1,3},{2,4},{3,5},{4,6},{5,7},{6,0},{7,1},{8,10},{9,11},{10,... | collective-permute-start | bytes 786440 | tf_op jit(solution)/shard_map/ppermute | solution.py:429
  51.8 9.5 %collective-permute-start.15 = (bf16[512,256]{1,0:T(8,128)(2,1)S(1)}, bf16[512,256]{1,0:T(8,128)(2,1)S(1)}, u32[]{:S(2)}, u32[]{:S(2)}) collective-permute-start(bf16[512,256]{1,0:T(8,128)(2,1)S(1)} %get-tuple-element.116), channel_id=1, source_target_pairs={{0,6},{1,7},{2,0},{3,1},{4,2},{5,3},{6,4},{7,5},{8,14},{9,15},{10,... | collective-permute-start | bytes 786440 | tf_op jit(solution)/shard_map/ppermute | solution.py:429
  56.0 10.6 %collective-permute-start.11 = (bf16[512,256]{1,0:T(8,128)(2,1)S(1)}, bf16[512,256]{1,0:T(8,128)(2,1)S(1)}, u32[]{:S(2)}, u32[]{:S(2)}) collective-permute-start(bf16[512,256]{1,0:T(8,128)(2,1)S(1)} %get-tuple-element.111), channel_id=1, source_target_pairs={{0,2},{1,3},{2,4},{3,5},{4,6},{5,7},{6,0},{7,1},{8,10},{9,11},{10,... | collective-permute-start | bytes 786440 | tf_op jit(solution)/shard_map/ppermute | solution.py:429
  56.7 10.0 %collective-permute-start.12 = (bf16[512,256]{1,0:T(8,128)(2,1)S(1)}, bf16[512,256]{1,0:T(8,128)(2,1)S(1)}, u32[]{:S(2)}, u32[]{:S(2)}) collective-permute-start(bf16[512,256]{1,0:T(8,128)(2,1)S(1)} %get-tuple-element.112), channel_id=1, source_target_pairs={{0,6},{1,7},{2,0},{3,1},{4,2},{5,3},{6,4},{7,5},{8,14},{9,15},{10,... | collective-permute-start | bytes 786440 | tf_op jit(solution)/shard_map/ppermute | solution.py:429
  61.5 24.1 %collective-permute-start.16 = (bf16[1024,256]{1,0:T(8,128)(2,1)S(1)}, bf16[1024,256]{1,0:T(8,128)(2,1)S(1)}, u32[]{:S(2)}, u32[]{:S(2)}) collective-permute-start(bf16[1024,256]{1,0:T(8,128)(2,1)S(1)} %get-tuple-element.119), channel_id=1, source_target_pairs={{0,6},{1,7},{2,0},{3,1},{4,2},{5,3},{6,4},{7,5},{8,14},{9,15},{10,... | collective-permute-start | bytes 1572872 | tf_op jit(solution)/shard_map/ppermute | solution.py:429
  63.4 22.2 %collective-permute-start.17 = (bf16[1024,256]{1,0:T(8,128)(2,1)S(1)}, bf16[1024,256]{1,0:T(8,128)(2,1)S(1)}, u32[]{:S(2)}, u32[]{:S(2)}) collective-permute-start(bf16[1024,256]{1,0:T(8,128)(2,1)S(1)} %get-tuple-element.121), channel_id=1, source_target_pairs={{0,2},{1,3},{2,4},{3,5},{4,6},{5,7},{6,0},{7,1},{8,10},{9,11},{10,... | collective-permute-start | bytes 1572872 | tf_op jit(solution)/shard_map/ppermute | solution.py:429
  63.6 19.0 %collective-permute-start.19 = (bf16[512,256]{1,0:T(8,128)(2,1)S(1)}, bf16[512,256]{1,0:T(8,128)(2,1)S(1)}, u32[]{:S(2)}, u32[]{:S(2)}) collective-permute-start(bf16[512,256]{1,0:T(8,128)(2,1)S(1)} %get-tuple-element.124), channel_id=1, source_target_pairs={{0,6},{1,7},{2,0},{3,1},{4,2},{5,3},{6,4},{7,5},{8,14},{9,15},{10,... | collective-permute-start | bytes 786440 | tf_op jit(solution)/shard_map/ppermute | solution.py:429
  66.7 18.9 %collective-permute-start.20 = (bf16[512,256]{1,0:T(8,128)(2,1)S(1)}, bf16[512,256]{1,0:T(8,128)(2,1)S(1)}, u32[]{:S(2)}, u32[]{:S(2)}) collective-permute-start(bf16[512,256]{1,0:T(8,128)(2,1)S(1)} %get-tuple-element.126), channel_id=1, source_target_pairs={{0,2},{1,3},{2,4},{3,5},{4,6},{5,7},{6,0},{7,1},{8,10},{9,11},{10,... | collective-permute-start | bytes 786440 | tf_op jit(solution)/shard_map/ppermute | solution.py:429
  66.8 21.9 %collective-permute-start.13 = (bf16[512,256]{1,0:T(8,128)(2,1)S(1)}, bf16[512,256]{1,0:T(8,128)(2,1)S(1)}, u32[]{:S(2)}, u32[]{:S(2)}) collective-permute-start(bf16[512,256]{1,0:T(8,128)(2,1)S(1)} %get-tuple-element.113), channel_id=1, source_target_pairs={{0,2},{1,3},{2,4},{3,5},{4,6},{5,7},{6,0},{7,1},{8,10},{9,11},{10,... | collective-permute-start | bytes 786440 | tf_op jit(solution)/shard_map/ppermute | solution.py:429
  82.7 7.6 %collective-permute-start.18 = (bf16[512,256]{1,0:T(8,128)(2,1)S(1)}, bf16[512,256]{1,0:T(8,128)(2,1)S(1)}, u32[]{:S(2)}, u32[]{:S(2)}) collective-permute-start(bf16[512,256]{1,0:T(8,128)(2,1)S(1)} %get-tuple-element.122), channel_id=1, source_target_pairs={{0,6},{1,7},{2,0},{3,1},{4,2},{5,3},{6,4},{7,5},{8,14},{9,15},{10,... | collective-permute-start | bytes 786440 | tf_op jit(solution)/shard_map/ppermute | solution.py:429
